TPU v7x, 512 devices: a whole 4x8x8 slice. The times are simulated.
512 devices in a mesh: leaf: 32 (over y, x), col: 16 (over z, core).
Axes of the slice: x: 4, y: 8, z: 8, core: 2. Of those that a mesh axis runs over, the one named last changes fastest.
Arguments:
- points: float32 [3, 262144], P(None, ('leaf', 'col'))
- point_ids: int32 [262144], P(('leaf', 'col')), may hold values from 0 to 1048575, as said below
- signs: int32 [262144], P(('leaf', 'col')), may hold values from 0 to 1
- hadamard_sample_rows: int32 [512], replicated, may hold values from 0 to 1048575, as said below
- samples: bfloat16 [262144, 512], P(('leaf', 'col')), may hold values from -6 to 6
- skeleton: int32 [60, 128], replicated, may hold values from 0 to 8191, as said below
- ranks: int32 [60], replicated, may hold values from 64 to 128, as said below
Outputs:
- leaf_basis: bfloat16 [262144, 128], P(('leaf', 'col'))
- top_sample: float32 [512, 512], P('leaf', 'col')
- top_omega: float32 [512, 512], P('leaf', 'col')
Inputs may be any that keep to these rules, and one draw needn't show every extreme that they name: `point_ids`: increasing and distinct; the first is 0 and the last 1048575. `hadamard_sample_rows`: increasing and distinct; the first is 0 and the last 1048575. `skeleton`: each row holds distinct indices; in the first 32 rows (leaves) they are below 8192, in the others below 256; entry i of a leaf row lies in [i * 64, (i + 1) * 64). `ranks`: some node has rank 128 and some other node rank 128 / 2.
All inputs are finite; a program needn't handle non-finite values.
Results may differ from a plain program's by a relative error of at most 0.0018.
Values sent between devices are 32-bit elements; how exact they have to be, the bound alone decides.
A program may use at most 64 MiB of HBM per device.

v0:
```python
import jax
import jax.numpy as jnp
from jax import lax
from jax.sharding import PartitionSpec as P

NTOTAL = 1048576


KERNEL_SCALE = 1.0
OMEGA_UNIT = 0.0625
RIDGE = 0.25
HIGH = lax.Precision.HIGHEST


def swapped(value, axis, bit):
    mask = 2**bit
    pairs = [(source, source ^ mask) for source in range(lax.axis_size(axis))]
    return lax.ppermute(value, axis, pairs)


def omega_rows(tags, hadamard_sample_rows, bit_count):
    powers = jnp.array([1 << shift for shift in range(bit_count)], dtype=jnp.int32)
    row_bits = (tags[0][:, None] // powers[None, :] % 2).astype(jnp.float32)
    col_bits = (hadamard_sample_rows[None, :] // powers[:, None] % 2).astype(jnp.float32)
    counted = jnp.dot(row_bits, col_bits, precision=HIGH)
    parity = counted - 2.0 * jnp.floor(0.5 * counted)
    flips = (2 * tags[1] - 1).astype(jnp.float32)
    return (1.0 - 2.0 * parity) * flips[:, None] * OMEGA_UNIT


def kernel_tile(left, right):
    squared_distance = jnp.zeros((left.shape[1], right.shape[1]), jnp.float32)
    for axis_k in range(3):
        offset = left[axis_k][:, None] - right[axis_k][None, :]
        squared_distance = squared_distance + offset * offset
    return jnp.exp(-KERNEL_SCALE * squared_distance)


def ridge_fit(picked, gram, rank):
    shift = RIDGE * jnp.trace(gram) / rank.astype(jnp.float32) + 1e-06
    ident = jnp.eye(gram.shape[0], dtype=jnp.float32)
    factor = jnp.linalg.cholesky(gram + shift * ident)
    return jax.scipy.linalg.cho_solve((factor, True), picked)


def local(points, point_ids, signs, hadamard_sample_rows, samples, skeleton, ranks):
    leaf_count = lax.axis_size("leaf")
    col_count = lax.axis_size("col")
    leaf_pos = lax.axis_index("leaf")
    col_pos = lax.axis_index("col")
    rows = points.shape[1]
    width = samples.shape[1]
    rank_limit = skeleton.shape[1]
    bit_count = NTOTAL.bit_length() - 1
    tags = jnp.stack([point_ids, signs])
    own_omega = omega_rows(tags, hadamard_sample_rows, bit_count)
    distant_points = lax.all_gather(points, "col", axis=1, tiled=True)
    far_tags = lax.all_gather(tags, "col", axis=1, tiled=True)
    block_omega = omega_rows(far_tags, hadamard_sample_rows, bit_count).astype(jnp.bfloat16)
    tile = kernel_tile(points, distant_points).astype(jnp.bfloat16)
    near = jnp.dot(tile, block_omega, preferred_element_type=jnp.float32)
    residue = samples.astype(jnp.float32) - near
    positions = jnp.arange(rank_limit, dtype=jnp.int32)
    leaf_skel = skeleton[leaf_pos] - col_pos * rows
    leaf_rank = ranks[leaf_pos]
    keep = (positions < leaf_rank).astype(jnp.float32)
    chooser = (leaf_skel[:, None] == jnp.arange(rows, dtype=jnp.int32)[None, :]).astype(jnp.float32)
    part_picked = jnp.dot(chooser, residue, precision=HIGH) * keep[:, None]
    part_spots = jnp.dot(points, chooser.T, precision=HIGH)
    picked, spots = lax.psum((part_picked, part_spots), "col")
    gram = jnp.dot(picked, picked.T, precision=HIGH)
    fitted = ridge_fit(picked, gram, leaf_rank)
    basis = jnp.dot(residue, fitted.T, precision=HIGH)
    projected = lax.psum(jnp.dot(basis.T, own_omega, precision=HIGH), "col")
    leaf_basis = basis.astype(jnp.bfloat16)
    span = width // col_count
    base = 0
    for level in range(1, 4):
        child_base = base
        base = base + (leaf_count >> level - 1)
        sibling_selected, other_proj, other_spots = swapped(
            (picked, projected, spots), "leaf", level - 1
        )
        is_left = leaf_pos // (1 << level - 1) % 2 == 0
        left_picked = jnp.where(is_left, picked, sibling_selected)
        right_picked = jnp.where(is_left, sibling_selected, picked)
        left_proj = jnp.where(is_left, projected, other_proj)
        right_proj = jnp.where(is_left, other_proj, projected)
        left_positions = jnp.where(is_left, spots, other_spots)
        right_spots = jnp.where(is_left, other_spots, spots)
        pair_index = leaf_pos // (1 << level)
        left_keep = (positions < ranks[child_base + 2 * pair_index]).astype(jnp.float32)
        right_keep = (positions < ranks[child_base + 2 * pair_index + 1]).astype(jnp.float32)
        cross = kernel_tile(left_positions, right_spots)
        upper = (left_picked - jnp.dot(cross, right_proj, precision=HIGH)) * left_keep[:, None]
        lower = (right_picked - jnp.dot(cross.T, left_proj, precision=HIGH)) * right_keep[:, None]
        candidates = jnp.concatenate([upper, lower], 0)
        stacked = jnp.concatenate([left_proj, right_proj], 0)
        cand_spots = jnp.concatenate([left_positions, right_spots], 1)
        node_skel = skeleton[base + pair_index]
        node_rank = ranks[base + pair_index]
        node_keep = (positions < node_rank).astype(jnp.float32)
        selector = (
            node_skel[:, None] == jnp.arange(2 * rank_limit, dtype=jnp.int32)[None, :]
        ).astype(jnp.float32)
        new_picked = jnp.dot(selector, candidates, precision=HIGH) * node_keep[:, None]
        new_spots = jnp.dot(cand_spots, selector.T, precision=HIGH)
        gram = jnp.dot(new_picked, new_picked.T, precision=HIGH)
        fitted = ridge_fit(new_picked, gram, node_rank)
        parent_basis = jnp.dot(candidates, fitted.T, precision=HIGH)
        projected = jnp.dot(parent_basis.T, stacked, precision=HIGH)
        picked = new_picked
        spots = new_spots
    picked = lax.dynamic_slice_in_dim(picked, col_pos * span, span, 1)
    projected = lax.dynamic_slice_in_dim(projected, col_pos * span, span, 1)
    share = rank_limit // 8
    top_sample = lax.dynamic_slice_in_dim(picked, leaf_pos % 8 * share, share, 0)
    top_omega = lax.dynamic_slice_in_dim(projected, leaf_pos % 8 * share, share, 0)
    return (leaf_basis, top_sample, top_omega)


def solution(mesh):
    placed = (
        P(None, ("leaf", "col")),
        P(("leaf", "col")),
        P(("leaf", "col")),
        P(),
        P(("leaf", "col"), None),
        P(),
        P(),
    )
    return jax.shard_map(
        local,
        mesh=mesh,
        in_specs=placed,
        out_specs=(P(("leaf", "col"), None), P("leaf", "col"), P("leaf", "col")),
        check_vma=False,
    )
```

profile of v0, /device:TPU:1, one launch (start us, length us, event | category | flops | bytes accessed | tf_op | source)
XLA Modules:
  0.0 487.4 jit_solution(7445075124836231805)
XLA Ops:
  7.2 25.1 %all_gather.6 = f32[3,8192]{1,0:T(4,128)S(1)} all-gather(f32[3,512]{1,0:T(4,128)} %param.14), channel_id=1, replica_groups=mesh['leaf'=32,'col'=16] {'col'}, dimensions={1}, use_global_device_ids=true | all-gather | bytes 104448 | tf_op jit(solution)/shard_map/all_gather | solution.py:57
  32.3 0.8 fusion.198
  33.1 0.7 pad_add_fusion
  33.8 14.6 %all_gather.7 = s32[2,8192]{1,0:T(2,128)S(1)} all-gather(s32[2,512]{1,0:T(2,128)S(1)} %pad_add_fusion), channel_id=1, replica_groups=mesh['leaf'=32,'col'=16] {'col'}, dimensions={1}, use_global_device_ids=true | all-gather | bytes 69632 | tf_op jit(solution)/shard_map/all_gather | solution.py:58
  48.5 0.7 compare_reduce_fusion
  49.4 1.7 fusion.199
  51.1 0.7 compare_convert_fusion.9
  51.8 0.8 fusion.165
  52.5 29.2 %multiply_convert_fusion = bf16[8192,512]{1,0:T(8,128)(2,1)S(1)} fusion(f32[8192]{0:T(1024)S(1)} %bitcast.150, s32[20]{0:T(128)} %constant.260.clone, s32[8192]{0:T(1024)S(1)} %bitcast.146, pred[8192]{0:T(1024)(128)(4,1)S(1)} %sign_compare_fusion, s32[512]{0:T(512)} %param.17, pred[512]{0:T(512)(128)(4,1)S(1)} %compare_reduce_fusion), kind=kOutput, calls=%fused_computation | convolution fusion | flops 1047515136 | bytes 8464976 | tf_op jit(solution)/shard_map/dot_general | solution.py:25
  81.8 6.7 %fusion.8 = f32[512,512]{1,0:T(8,128)S(1)} fusion(bf16[8192,512]{1,0:T(8,128)(2,1)S(1)} %multiply_convert_fusion, f32[8192]{0:T(1024)S(1)} %bitcast.148, f32[512]{0:T(512)S(1)} %bitcast.156, f32[8192]{0:T(1024)S(1)} %bitcast.149, f32[512]{0:T(512)S(1)} %bitcast.155, f32[8192]{0:T(1024)S(1)} %bitcast.147, f32[512]{0:T(512)S(1)} %bitcast.154, ...), kind=kOutput, calls=%fused_computation.10 | convolution fusion | flops 4337434624 | bytes 10065920 | tf_op jit(solution)/shard_map/dot_general | solution.py:61
  88.5 1.2 convolution_multiply_fusion.3
  90.1 23.1 %psum.22 = f32[3,128]{1,0:T(4,128)S(1)} all-reduce(f32[3,128]{1,0:T(4,128)S(1)} %convolution_bitcast_fusion), channel_id=1, replica_groups=mesh['leaf'=32,'col'=16] {'col'}, use_global_device_ids=true, to_apply=%region_4.8 | all-reduce | flops 384 | bytes 3072 | tf_op jit(solution)/shard_map/psum | solution.py:70
  113.2 3.5 collective-permute-start.1
  119.4 4.1 fusion.54
  124.1 0.7 compare_convert_fusion.4
  126.0 0.7 compare_convert_fusion.1
  129.4 73.6 %all-reduce.3.cloned.1.call-done = f32[128,512]{1,0:T(8,128)} async-done(((f32[128,512]{1,0:T(8,128)}), f32[128,512]{1,0:T(8,128)}) %all-reduce.3.cloned.1.call-update) | async-done | bytes 262160 | tf_op jit(solution)/shard_map/psum | solution.py:70
  203.0 2.1 select_reduce_fusion.7
  205.9 11.7 %cholesky.74 = f32[128,128]{1,0:T(8,128)S(1)} custom-call(f32[128,128]{1,0:T(8,128)S(1)} %fusion.94), custom_call_target="Cholesky" | custom-call | tf_op jit(solution)/shard_map/jit(cholesky)/cholesky | solution.py:42
  219.0 9.8 %custom-call.10 = f32[1,128,128]{1,2,0:T(8,128)S(1)} custom-call(f32[1,128,128]{2,1,0:T(8,128)S(1)} %fusion.71), custom_call_target="InvertDiagBlocksLowerTriangular" | custom-call | tf_op jit(solution)/shard_map/jit(_cho_solve)/triangular_solve | solution.py:43
  228.8 1.4 fusion.92
  230.6 1.8 fusion.200
  232.4 1.8 fusion.9
  234.4 4.7 collective-permute-start.4
  239.1 111.2 %all-reduce.5.cloned.1.call-done = f32[128,512]{1,0:T(8,128)} async-done(((f32[128,512]{1,0:T(8,128)}), f32[128,512]{1,0:T(8,128)}) %all-reduce.5.cloned.1.call-update) | async-done | bytes 262160 | tf_op jit(solution)/shard_map/psum | solution.py:74
  350.2 3.1 collective-permute-start.2
  353.4 2.2 collective-permute-start
  355.6 4.0 collective-permute-done.2
  359.6 1.0 broadcast_select_fusion.1
  360.6 4.6 collective-permute-done
  366.6 1.0 select_reduce_fusion.6
  368.4 11.7 %cholesky.85 = f32[128,128]{1,0:T(8,128)S(1)} custom-call(f32[128,128]{1,0:T(8,128)S(1)} %fusion.89), custom_call_target="Cholesky" | custom-call | tf_op jit(solution)/shard_map/jit(cholesky)/cholesky | solution.py:42
  381.4 9.8 %custom-call.11 = f32[1,128,128]{1,2,0:T(8,128)S(1)} custom-call(f32[1,128,128]{2,1,0:T(8,128)S(1)} %fusion.72), custom_call_target="InvertDiagBlocksLowerTriangular" | custom-call | tf_op jit(solution)/shard_map/jit(_cho_solve)/triangular_solve | solution.py:43
  393.1 4.6 collective-permute-start.5
  397.7 2.2 collective-permute-start.3
  400.1 3.4 collective-permute-start.7
  403.6 5.7 %collective-permute-done.3 = f32[128,512]{1,0:T(8,128)S(1)} collective-permute-done((f32[128,512]{1,0:T(8,128)S(1)}, f32[128,512]{1,0:T(8,128)S(1)}, u32[]{:S(2)}, u32[]{:S(2)}) %collective-permute-start.3) | collective-permute-done | bytes 262176 | tf_op jit(solution)/shard_map/ppermute | solution.py:18
  410.6 1.0 select_reduce_fusion.5
  412.4 11.7 %cholesky.96 = f32[128,128]{1,0:T(8,128)S(1)} custom-call(f32[128,128]{1,0:T(8,128)S(1)} %fusion.84), custom_call_target="Cholesky" | custom-call | tf_op jit(solution)/shard_map/jit(cholesky)/cholesky | solution.py:42
  425.4 9.8 %custom-call.12 = f32[1,128,128]{1,2,0:T(8,128)S(1)} custom-call(f32[1,128,128]{2,1,0:T(8,128)S(1)} %fusion.73), custom_call_target="InvertDiagBlocksLowerTriangular" | custom-call | tf_op jit(solution)/shard_map/jit(_cho_solve)/triangular_solve | solution.py:43
  437.1 3.1 collective-permute-start.8
  440.3 2.4 collective-permute-start.6
  442.7 2.6 collective-permute-done.8
  445.3 5.6 %collective-permute-done.6 = f32[128,512]{1,0:T(8,128)S(1)} collective-permute-done((f32[128,512]{1,0:T(8,128)S(1)}, f32[128,512]{1,0:T(8,128)S(1)}, u32[]{:S(2)}, u32[]{:S(2)}) %collective-permute-start.6) | collective-permute-done | bytes 262176 | tf_op jit(solution)/shard_map/ppermute | solution.py:18
  452.2 1.0 select_reduce_fusion.4
  454.0 11.7 %cholesky.107 = f32[128,128]{1,0:T(8,128)S(1)} custom-call(f32[128,128]{1,0:T(8,128)S(1)} %fusion.79), custom_call_target="Cholesky" | custom-call | tf_op jit(solution)/shard_map/jit(cholesky)/cholesky | solution.py:42
  467.1 9.8 %custom-call.13 = f32[1,128,128]{1,2,0:T(8,128)S(1)} custom-call(f32[1,128,128]{2,1,0:T(8,128)S(1)} %fusion.74), custom_call_target="InvertDiagBlocksLowerTriangular" | custom-call | tf_op jit(solution)/shard_map/jit(_cho_solve)/triangular_solve | solution.py:43
  478.7 0.7 dynamic_slice.64
  (92 shorter events, 21.7 us)
Async XLA Ops:
  7.2 195.8 %all-reduce.3.cloned.1.call-start = ((), (), s32[]{:S(2)}) async-start(), calls=%async_computation | async-start | bytes 524288 | tf_op jit(solution)/shard_map/psum | solution.py:70
  52.5 29.2 %copy-start.5 = (bf16[512,512]{1,0:T(8,128)(2,1)S(1)}, bf16[512,512]{1,0:T(8,128)(2,1)}, u32[]{:S(2)}) copy-start(bf16[512,512]{1,0:T(8,128)(2,1)} %param.18) | copy-start | bytes 1572868
  81.8 8.1 %copy-start.1 = (f32[3,512]{1,0:T(4,128)S(1)}, f32[3,512]{1,0:T(4,128)}, u32[]{:S(2)}) copy-start(f32[3,512]{1,0:T(4,128)} %param.14) | copy-start | bytes 18436
  81.8 35.7 %copy-start.2 = (s32[512]{0:T(512)S(1)}, s32[512]{0:T(512)}, u32[]{:S(2)}) copy-start(s32[512]{0:T(512)} %param.15) | copy-start | bytes 6148
  81.8 35.7 %copy-start.3 = (s32[512]{0:T(512)S(1)}, s32[512]{0:T(512)}, u32[]{:S(2)}) copy-start(s32[512]{0:T(512)} %param.16) | copy-start | bytes 6148
  81.8 37.6 %copy-start.4 = (s32[512]{0:T(512)S(1)}, s32[512]{0:T(512)}, u32[]{:S(2)}) copy-start(s32[512]{0:T(512)} %param.17) | copy-start | bytes 6148
  81.8 37.6 %copy-start.6 = (s32[20]{0:T(128)S(1)}, s32[20]{0:T(128)}, u32[]{:S(2)}) copy-start(s32[20]{0:T(128)} %constant.260.clone) | copy-start | bytes 244
  89.8 260.5 %all-reduce.5.cloned.1.call-start = ((), (), s32[]{:S(2)}) async-start(), calls=%async_computation.1 | async-start | bytes 524288 | tf_op jit(solution)/shard_map/psum | solution.py:74
  113.2 16.2 %collective-permute-start.1 = (f32[3,128]{1,0:T(4,128)S(1)}, f32[3,128]{1,0:T(4,128)S(1)}, u32[]{:S(2)}, u32[]{:S(2)}) collective-permute-start(f32[3,128]{1,0:T(4,128)S(1)} %psum.22), channel_id=1, source_target_pairs={{0,16},{16,0},{32,48},{48,32},{64,80},{80,64},{96,112},{112,96},{1... | collective-permute-start | bytes 4616 | tf_op jit(solution)/shard_map/ppermute | solution.py:18
  203.0 162.7 %copy-start = (f32[128,512]{1,0:T(8,128)S(1)}, f32[128,512]{1,0:T(8,128)}, u32[]{:S(2)}) copy-start(f32[128,512]{1,0:T(8,128)} %all-reduce.3.cloned.1.call-done) | copy-start | bytes 786436
  234.4 121.2 %collective-permute-start.4 = (f32[3,128]{1,0:T(4,128)S(1)}, f32[3,128]{1,0:T(4,128)S(1)}, u32[]{:S(2)}, u32[]{:S(2)}) collective-permute-start(f32[3,128]{1,0:T(4,128)S(1)} %fusion.66), channel_id=1, source_target_pairs={{0,32},{16,48},{32,0},{48,16},{64,96},{80,112},{96,64},{112,80},{1... | collective-permute-start | bytes 4616 | tf_op jit(solution)/shard_map/ppermute | solution.py:18
  350.2 9.3 %collective-permute-start.2 = (f32[128,512]{1,0:T(8,128)}, f32[128,512]{1,0:T(8,128)S(1)}, u32[]{:S(2)}, u32[]{:S(2)}) collective-permute-start(f32[128,512]{1,0:T(8,128)} %all-reduce.5.cloned.1.call-done), channel_id=1, source_target_pairs={{0,16},{16,0},{32,48},{48,32},{64,80},{80,64},{96,112},{112,96},{1... | collective-permute-start | bytes 786440 | tf_op jit(solution)/shard_map/ppermute | solution.py:18
  353.4 11.8 %collective-permute-start = (f32[128,512]{1,0:T(8,128)}, f32[128,512]{1,0:T(8,128)S(1)}, u32[]{:S(2)}, u32[]{:S(2)}) collective-permute-start(f32[128,512]{1,0:T(8,128)} %all-reduce.3.cloned.1.call-done), channel_id=1, source_target_pairs={{0,16},{16,0},{32,48},{48,32},{64,80},{80,64},{96,112},{112,96},{1... | collective-permute-start | bytes 786440 | tf_op jit(solution)/shard_map/ppermute | solution.py:18
  393.1 10.4 %collective-permute-start.5 = (f32[128,512]{1,0:T(8,128)S(1)}, f32[128,512]{1,0:T(8,128)S(1)}, u32[]{:S(2)}, u32[]{:S(2)}) collective-permute-start(f32[128,512]{1,0:T(8,128)S(1)} %fusion.25), channel_id=1, source_target_pairs={{0,32},{16,48},{32,0},{48,16},{64,96},{80,112},{96,64},{112,80},{1... | collective-permute-start | bytes 786440 | tf_op jit(solution)/shard_map/ppermute | solution.py:18
  397.7 11.5 %collective-permute-start.3 = (f32[128,512]{1,0:T(8,128)S(1)}, f32[128,512]{1,0:T(8,128)S(1)}, u32[]{:S(2)}, u32[]{:S(2)}) collective-permute-start(f32[128,512]{1,0:T(8,128)S(1)} %convolution_multiply_fusion.2), channel_id=1, source_target_pairs={{0,32},{16,48},{32,0},{48,16},{64,96},{80,112},{96,64},{112,80},{1... | collective-permute-start | bytes 786440 | tf_op jit(solution)/shard_map/ppermute | solution.py:18
  400.1 40.1 %collective-permute-start.7 = (f32[3,128]{1,0:T(4,128)S(1)}, f32[3,128]{1,0:T(4,128)S(1)}, u32[]{:S(2)}, u32[]{:S(2)}) collective-permute-start(f32[3,128]{1,0:T(4,128)S(1)} %fusion.67), channel_id=1, source_target_pairs={{0,64},{16,80},{32,96},{48,112},{64,0},{80,16},{96,32},{112,48},{1... | collective-permute-start | bytes 4616 | tf_op jit(solution)/shard_map/ppermute | solution.py:18
  437.1 8.1 %collective-permute-start.8 = (f32[128,512]{1,0:T(8,128)S(1)}, f32[128,512]{1,0:T(8,128)S(1)}, u32[]{:S(2)}, u32[]{:S(2)}) collective-permute-start(f32[128,512]{1,0:T(8,128)S(1)} %fusion.29), channel_id=1, source_target_pairs={{0,64},{16,80},{32,96},{48,112},{64,0},{80,16},{96,32},{112,48},{1... | collective-permute-start | bytes 786440 | tf_op jit(solution)/shard_map/ppermute | solution.py:18
  440.3 10.6 %collective-permute-start.6 = (f32[128,512]{1,0:T(8,128)S(1)}, f32[128,512]{1,0:T(8,128)S(1)}, u32[]{:S(2)}, u32[]{:S(2)}) collective-permute-start(f32[128,512]{1,0:T(8,128)S(1)} %convolution_multiply_fusion.1), channel_id=1, source_target_pairs={{0,64},{16,80},{32,96},{48,112},{64,0},{80,16},{96,32},{112,48},{1... | collective-permute-start | bytes 786440 | tf_op jit(solution)/shard_map/ppermute | solution.py:18
Sparse Core Ops, SparseCore 0:
  89.9 113.0 all-reduce.2
  234.3 115.8 all-reduce.4
where the time goes:
time: 496 us; the launch traced here: 487 us
  waiting for transfers between devices  207 us (42%)
  other arithmetic  101 us (20%)
  blocking collectives  62.8 us (13%)
  matrix products  61.6 us (12%)
  starting transfers between devices  29.2 us (6%)
  between operations  20.8 us (4%)
    psum x1, waiting for transfers between devices, local(): projected = lax.psum(jnp.dot(basis.T, own_omega, precision=HIGH), 'col')  111 us
    psum x1, waiting for transfers between devices, local(): picked, spots = lax.psum((part_picked, part_spots), 'col')  73.6 us
    another operation x12, other arithmetic, ridge_fit(): factor = jnp.linalg.cholesky(gram + shift * ident)  49.6 us
    another operation x8, other arithmetic, ridge_fit(): return jax.scipy.linalg.cho_solve((factor, True), picked)  41.9 us
    dot_general x2, matrix products, omega_rows(): counted = jnp.dot(row_bits, col_bits, precision=HIGH)  33.3 us
    ppermute x9, starting transfers between devices, swapped(): return lax.ppermute(value, axis, pairs)  29.2 us
    all_gather x1, blocking collectives, local(): distant_points = lax.all_gather(points, 'col', axis=1, tiled=True)  25.1 us
    psum x1, blocking collectives, local(): picked, spots = lax.psum((part_picked, part_spots), 'col')  23.1 us
  transfers between devices with their start and end apart: 11, of which 7 were waited for; matrix products, arithmetic and copies ran while one was open for 8% of the time, Pallas kernels for 0%

commit v1 on v0

v1 whole, which is shorter than its diff:
```python
import functools

import jax
import jax.numpy as jnp
from jax import lax
from jax.experimental import pallas as pl
from jax.experimental.pallas import tpu as pltpu
from jax.sharding import PartitionSpec as P

MESH = pl.DeviceIdType.MESH
HIGH = lax.Precision.HIGHEST
F32 = jnp.float32
BF16 = jnp.bfloat16
VM = pl.BlockSpec(memory_space=pltpu.VMEM)
SM = pl.BlockSpec(memory_space=pltpu.SMEM)

NTOTAL = 1048576
KERNEL_SCALE = 1.0
RIDGE = 0.25
LOG2E = 1.4426950408889634
BITS = NTOTAL.bit_length() - 1
PANEL = 16
COLS = 16
LANES = 128


def dot(a, b, ca, cb, precision=HIGH):
    return lax.dot_general(
        a, b, (((ca,), (cb,)), ((), ())), precision=precision, preferred_element_type=F32
    )


def split3(x):
    hi = x.astype(BF16)
    rest = x - hi.astype(F32)
    mid = rest.astype(BF16)
    low = (rest - mid.astype(F32)).astype(BF16)
    return hi, mid, low


def iota(shape, axis):
    return lax.broadcasted_iota(jnp.int32, shape, axis)


def kern(squared_distance):
    return jnp.exp2(squared_distance * (-KERNEL_SCALE * LOG2E))


def spd_inverse(a_ref):
    n = a_ref.shape[0]
    lane = iota((PANEL, n), 1)
    sub = iota((PANEL, n), 0)
    ident = (lane == sub).astype(F32)
    lane_n = iota((n, n), 1)

    def step(b, carry):
        start = pl.multiple_of(b * PANEL, PANEL)
        panel = a_ref[pl.ds(start, PANEL), :]
        rolled = pltpu.roll(panel, lax.rem(n - start, n), 1)
        diag = [jnp.broadcast_to(rolled[:, k : k + 1], (PANEL, n)) for k in range(PANEL)]
        rows = jnp.where(lane < PANEL, ident, rolled)
        for k in range(PANEL):
            inv = 1.0 / diag[k][k : k + 1, :]
            here = sub == k
            factor = diag[k] * inv
            for j in range(k + 1, PANEL):
                own = diag[j][k : k + 1, :]
                diag[j] = jnp.where(here, own * inv, diag[j] - factor * own)
            own = rows[k : k + 1, :]
            rows = jnp.where(here, own * inv, rows - factor * own)
        rows = pltpu.roll(rows, start, 1)
        side = jnp.where(lane < start, -panel, panel)
        side = jnp.where((lane >= start) & (lane < start + PANEL), 0.0, side)
        q1, q2, q3 = split3(side)
        r1, r2, r3 = split3(rows)
        left = jnp.concatenate([q1, q1, q1, q2, q2, q3], 0)
        right = jnp.concatenate([r1, r2, r3, r1, r2, r1], 0)
        change = dot(left, right, 0, 0, lax.Precision.DEFAULT)
        cleared = jnp.where((lane_n >= start) & (lane_n < start + PANEL), 0.0, a_ref[...])
        a_ref[...] = cleared - change
        a_ref[pl.ds(start, PANEL), :] = rows
        return carry

    lax.fori_loop(0, n // PANEL, step, 0)


def ridge_inverse(gram, rank, a_ref):
    n = gram.shape[0]
    same = iota((n, n), 0) == iota((n, n), 1)
    trace = jnp.sum(jnp.where(same, gram, 0.0), keepdims=True)
    shift = RIDGE * trace / rank.astype(F32) + 1e-06
    a_ref[...] = gram + jnp.where(same, shift, 0.0)
    spd_inverse(a_ref)


def gather_kernel(x_ref, o_ref, send, recv):
    me = lax.axis_index("col")
    barrier = pltpu.get_barrier_semaphore()
    for off in range(1, COLS):
        pl.semaphore_signal(
            barrier, inc=1, device_id={"col": lax.rem(me + off, COLS)}, device_id_type=MESH
        )
    pl.semaphore_wait(barrier, COLS - 1)
    copies = []
    for off in range(1, COLS):
        peer = lax.rem(me + off, COLS)
        copy = pltpu.make_async_remote_copy(
            src_ref=x_ref,
            dst_ref=o_ref.at[me],
            send_sem=send.at[off],
            recv_sem=recv.at[COLS - off],
            device_id={"col": peer},
            device_id_type=MESH,
        )
        copy.start()
        copies.append(copy)
    o_ref[me] = x_ref[...]
    for off in range(1, COLS):
        pltpu.make_async_remote_copy(
            src_ref=x_ref,
            dst_ref=o_ref.at[lax.rem(me + off, COLS)],
            send_sem=send.at[off],
            recv_sem=recv.at[off],
            device_id={"col": lax.rem(me + off, COLS)},
            device_id_type=MESH,
        ).wait_recv()
    for copy in copies:
        copy.wait_send()


def gather_cols(x, cid):
    return pl.pallas_call(
        gather_kernel,
        out_shape=jax.ShapeDtypeStruct((COLS, *x.shape), x.dtype),
        in_specs=[VM],
        out_specs=VM,
        scratch_shapes=[pltpu.SemaphoreType.DMA((COLS,)), pltpu.SemaphoreType.DMA((COLS,))],
        compiler_params=pltpu.CompilerParams(collective_id=cid, has_side_effects=True),
        name=f"gather_{cid}",
    )(x)


def reduce_kernel(n_ref, o_ref, half, mine, landed, s0, r0, s1, r1, s2, r2, s3, r3):
    me = lax.axis_index("col")
    core = lax.rem(me, 2)
    z = me // 2
    partner = me + 1 - 2 * core
    zs = COLS // 2
    rows = n_ref.shape[0]
    part = rows // 2
    piece = part // zs
    barrier = pltpu.get_barrier_semaphore()
    peers = [lax.rem(z + off, zs) * 2 + core for off in range(1, zs)]
    for peer in [partner, *peers]:
        pl.semaphore_signal(barrier, inc=1, device_id={"col": peer}, device_id_type=MESH)
    pl.semaphore_wait(barrier, zs)

    def copy(src, dst, send, recv, peer):
        return pltpu.make_async_remote_copy(
            src_ref=src,
            dst_ref=dst,
            send_sem=send,
            recv_sem=recv,
            device_id={"col": peer},
            device_id_type=MESH,
        )

    own0 = pl.multiple_of(core * part, part)
    other0 = pl.multiple_of((1 - core) * part, part)
    first = copy(n_ref.at[pl.ds(other0, part)], half, s0, r0, partner)
    first.start()
    first.wait_recv()
    mine[...] = n_ref[pl.ds(own0, part)] + half[...]
    waits = [first]
    for off in range(1, zs):
        peer = lax.rem(z + off, zs)
        put = copy(
            mine.at[pl.ds(pl.multiple_of(peer * piece, piece), piece)],
            landed.at[off - 1],
            s1.at[off - 1],
            r1.at[off - 1],
            peers[off - 1],
        )
        put.start()
        waits.append(put)
    here = pl.multiple_of(z * piece, piece)
    total = mine[pl.ds(here, piece)]
    for off in range(1, zs):
        waits[off].wait_recv()
        total = total + landed[off - 1]
    slot = pl.multiple_of(own0 + here, piece)
    o_ref[pl.ds(slot, piece)] = total
    spread = []
    for off in range(1, zs):
        put = copy(o_ref.at[pl.ds(slot, piece)], o_ref.at[pl.ds(slot, piece)], s2.at[off - 1], r2.at[off - 1], peers[off - 1])
        put.start()
        spread.append(put)
    put = copy(o_ref.at[pl.ds(slot, piece)], o_ref.at[pl.ds(slot, piece)], s3.at[0], r3.at[0], partner)
    put.start()
    relays = [put]
    for off in range(1, zs):
        spread[off - 1].wait_recv()
        source = lax.rem(z + zs - off, zs)
        rng = pl.ds(pl.multiple_of(own0 + source * piece, piece), piece)
        put = copy(o_ref.at[rng], o_ref.at[rng], s3.at[off], r3.at[off], partner)
        put.start()
        relays.append(put)
    for put in relays:
        put.wait_recv()
    for put in waits + spread + relays:
        put.wait_send()


def reduce_cols(x, cid):
    rows, width = x.shape
    zs = COLS // 2
    part = rows // 2
    dma = pltpu.SemaphoreType.DMA
    return pl.pallas_call(
        reduce_kernel,
        out_shape=jax.ShapeDtypeStruct(x.shape, x.dtype),
        in_specs=[VM],
        out_specs=VM,
        scratch_shapes=[
            pltpu.VMEM((part, width), F32),
            pltpu.VMEM((part, width), F32),
            pltpu.VMEM((zs - 1, part // zs, width), F32),
            dma(()),
            dma(()),
            dma((zs - 1,)),
            dma((zs - 1,)),
            dma((zs - 1,)),
            dma((zs - 1,)),
            dma((zs,)),
            dma((zs,)),
        ],
        compiler_params=pltpu.CompilerParams(collective_id=cid, has_side_effects=True),
        name=f"reduce_{cid}",
    )(x)


CHUNKS = 4


def swap_kernel(bit, *refs):
    n = 2
    ins, outs = refs[:n], refs[n : 2 * n]
    s1, r1, s2, r2 = refs[2 * n :]
    leaf = lax.axis_index("leaf")
    me = lax.axis_index("col")
    core = lax.rem(me, 2)
    partner = me + 1 - 2 * core
    side = lax.rem(leaf // bit, 2)
    sibling = leaf + bit - 2 * bit * side
    barrier = pltpu.get_barrier_semaphore()
    pl.semaphore_signal(barrier, inc=1, device_id={"leaf": sibling}, device_id_type=MESH)
    pl.semaphore_signal(barrier, inc=1, device_id={"col": partner}, device_id_type=MESH)
    pl.semaphore_wait(barrier, 2)
    rows = ins[0].shape[0]
    size = rows // 2 // CHUNKS
    first = []
    for i in range(n):
        for q in range(CHUNKS):
            rng = pl.ds(pl.multiple_of(core * (rows // 2) + q * size, size), size)
            put = pltpu.make_async_remote_copy(
                src_ref=ins[i].at[rng],
                dst_ref=outs[i].at[side, rng],
                send_sem=s1.at[i, q],
                recv_sem=r1.at[i, q],
                device_id={"leaf": sibling},
                device_id_type=MESH,
            )
            put.start()
            first.append(put)
    for i in range(n):
        outs[i][side] = ins[i][...]
    second = []
    for i in range(n):
        for q in range(CHUNKS):
            rng = pl.ds(pl.multiple_of(core * (rows // 2) + q * size, size), size)
            first[i * CHUNKS + q].wait_recv()
            put = pltpu.make_async_remote_copy(
                src_ref=outs[i].at[1 - side, rng],
                dst_ref=outs[i].at[1 - side, rng],
                send_sem=s2.at[i, q],
                recv_sem=r2.at[i, q],
                device_id={"col": partner},
                device_id_type=MESH,
            )
            put.start()
            second.append(put)
    for put in second:
        put.wait_recv()
    for put in first + second:
        put.wait_send()


def swap_siblings(xs, bit, cid):
    dma = pltpu.SemaphoreType.DMA
    n = len(xs)
    return pl.pallas_call(
        functools.partial(swap_kernel, bit),
        out_shape=[jax.ShapeDtypeStruct((2, *x.shape), x.dtype) for x in xs],
        in_specs=[VM] * n,
        out_specs=[VM] * n,
        scratch_shapes=[dma((n, CHUNKS))] * 4,
        compiler_params=pltpu.CompilerParams(collective_id=cid, has_side_effects=True),
        name=f"swap_{cid}",
    )(*xs)


def near_kernel(all_ref, own_ref, had_ref, samp_ref, skel_ref, rank_ref, res_ref, om_ref, pick_ref, acc, own_b, idx, sem):
    col = lax.axis_index("col")
    leaf = lax.axis_index("leaf")
    rows = own_ref.shape[1]
    width = samp_ref.shape[1]
    nbits = 32
    load = pltpu.make_async_copy(skel_ref.at[leaf], idx, sem)
    load.start()
    bit_row = iota((nbits, width), 0)
    had = jnp.broadcast_to(had_ref[...], (nbits, width))
    had_bits = ((had >> jnp.minimum(bit_row, BITS)) & 1).astype(F32) * 0.5
    had_bits = jnp.where(bit_row == BITS, 0.5, jnp.where(bit_row == BITS + 1, 0.25, had_bits))
    had_bits = jnp.where(bit_row > BITS + 1, 0.0, had_bits).astype(BF16)

    def omega4(block):
        shift = iota((nbits, rows), 0)
        ids = jnp.broadcast_to(block[3:4, :].astype(jnp.int32), (nbits, rows))
        bits = ((ids >> jnp.minimum(shift, BITS)) & 1).astype(F32)
        bits = jnp.where(shift == BITS, 1.0 - block[4:5, :], bits)
        bits = jnp.where(shift == BITS + 1, 1.0, bits)
        bits = jnp.where(shift > BITS + 1, 0.0, bits).astype(BF16)
        half = dot(bits, had_bits, 0, 0, lax.Precision.DEFAULT)
        return (half - jnp.round(half)).astype(BF16)

    own = own_ref[...]
    ident = (iota((8, LANES), 0) == iota((8, LANES), 1)).astype(F32)
    own_cols = dot(own, ident, 0, 0)
    for axis in range(3):
        own_b[axis] = jnp.broadcast_to(own_cols[:, axis : axis + 1], (rows, LANES))
    om_ref[...] = omega4(own)

    def step(j, carry):
        block = all_ref[j]
        om = omega4(block)
        tiles = []
        for c in range(rows // LANES):
            d2 = jnp.zeros((rows, LANES), F32)
            for axis in range(3):
                off = own_b[axis] - block[axis : axis + 1, c * LANES : (c + 1) * LANES]
                d2 = d2 + off * off
            tiles.append(kern(d2).astype(BF16))
        part = dot(jnp.concatenate(tiles, 1), om, 1, 0, lax.Precision.DEFAULT)

        @pl.when(j == 0)
        def _():
            acc[...] = part

        @pl.when(j > 0)
        def _():
            acc[...] += part

        return carry

    lax.fori_loop(0, COLS, step, 0)
    res_ref[...] = samp_ref[...].astype(F32) - 0.25 * acc[...]
    load.wait()
    count = pick_ref.shape[0]
    rank = rank_ref[leaf]
    acc[:, 0:LANES] = own_cols
    for i in range(count):
        entry = col * count + i
        where = idx[entry] - col * rows
        keep = jnp.where(entry < rank, 1.0, 0.0)
        tile = pl.ds(pl.multiple_of(where // 8 * 8, 8), 8)
        hit = iota((8, 1), 0) == lax.rem(where, 8)
        row = jnp.sum(jnp.where(hit, res_ref[tile, :], 0.0), 0, keepdims=True)
        pick_ref[i : i + 1, 0:width] = row * keep
        pick_ref[i : i + 1, width : width + LANES] = jnp.sum(
            jnp.where(hit, acc[tile, 0:LANES], 0.0), 0, keepdims=True
        )


def leaf_kernel(pick_ref, res_ref, om_ref, rank_ref, part_ref, basis_ref, inv_ref):
    leaf = lax.axis_index("leaf")
    width = res_ref.shape[1]
    picked = pick_ref[:, 0:width]
    gram = dot(picked, picked, 1, 1)
    raw = dot(res_ref[...], picked, 1, 1)
    om = om_ref[...]
    total = None
    for piece in split3(raw):
        term = dot(piece, om, 0, 0, lax.Precision.DEFAULT)
        total = term if total is None else total + term
    part_ref[...] = total * 0.25
    ridge_inverse(gram, rank_ref[leaf], inv_ref)
    basis_ref[...] = dot(raw, inv_ref[...], 1, 0).astype(BF16)


def merge_kernel(level, child_base, base, pk_ref, pr_ref, skel_ref, rank_ref, *refs):
    leaf = lax.axis_index("leaf")
    width = pr_ref.shape[2]
    r = pr_ref.shape[1]
    pair = leaf // (1 << level)
    rank_l = rank_ref[child_base + 2 * pair]
    rank_r = rank_ref[child_base + 2 * pair + 1]
    rank_p = rank_ref[base + pair]
    spots_l = pk_ref[0, :, width : width + LANES]
    spots_r = pk_ref[1, :, width : width + LANES]
    row_r = spots_r.T
    d2 = jnp.zeros((r, r), F32)
    for axis in range(3):
        off = spots_l[:, axis : axis + 1] - row_r[axis : axis + 1, :]
        d2 = d2 + off * off
    cross = kern(d2)
    proj_l, proj_r = pr_ref[0], pr_ref[1]
    sub = iota((r, 1), 0)
    upper = (pk_ref[0, :, 0:width] - dot(cross, proj_r, 1, 0)) * jnp.where(sub < rank_l, 1.0, 0.0)
    lower = (pk_ref[1, :, 0:width] - dot(cross, proj_l, 0, 0)) * jnp.where(sub < rank_r, 1.0, 0.0)
    cand = jnp.concatenate([upper, lower], 0)
    spots = jnp.concatenate([spots_l, spots_r], 0)
    row = skel_ref[pl.ds(base + pair, 1), :]
    chooser = jnp.where(jnp.broadcast_to(row, (2 * r, r)) == iota((2 * r, r), 0), 1.0, 0.0).astype(BF16)
    chosen = None
    for piece in split3(jnp.concatenate([cand, spots], 1)):
        term = dot(chooser, piece, 0, 0, lax.Precision.DEFAULT)
        chosen = term if chosen is None else chosen + term
    picked = chosen[:, 0:width] * jnp.where(sub < rank_p, 1.0, 0.0)
    gram = dot(picked, picked, 1, 1)
    raw = dot(cand, picked, 1, 1)
    back = dot(raw[0:r], proj_l, 0, 0) + dot(raw[r:], proj_r, 0, 0)
    if len(refs) == 3:
        out_pk, out_pr, inv_ref = refs
        out_pk[:, 0:width] = picked
        out_pk[:, width : width + LANES] = chosen[:, width : width + LANES]
        ridge_inverse(gram, rank_p, inv_ref)
        out_pr[...] = dot(inv_ref[...], back, 1, 0)
    else:
        top_s, top_o, inv_ref, tmp = refs
        col = lax.axis_index("col")
        share, span = top_s.shape
        ridge_inverse(gram, rank_p, inv_ref)
        tmp[...] = picked
        turn = lax.rem(width - col * span, width)
        rows = pl.ds(pl.multiple_of(lax.rem(leaf, 8) * share, share), share)
        top_s[...] = pltpu.roll(tmp[rows, :], turn, 1)[:, 0:span]
        mine = dot(inv_ref[rows, :], back, 1, 0)
        top_o[...] = pltpu.roll(mine, turn, 1)[:, 0:span]


def local(points, point_ids, signs, hadamard_sample_rows, samples, skeleton, ranks):
    rows = points.shape[1]
    width = samples.shape[1]
    r = skeleton.shape[1]
    leaf_count = lax.axis_size("leaf")
    own = jnp.concatenate(
        [
            points,
            point_ids[None].astype(F32),
            signs[None].astype(F32),
            jnp.zeros((3, rows), F32),
        ],
        0,
    )
    everyone = gather_cols(own, 0)
    shape = jax.ShapeDtypeStruct
    residue, om, picks = pl.pallas_call(
        near_kernel,
        out_shape=[shape((rows, width), F32), shape((rows, width), BF16), shape((r // COLS, width + LANES), F32)],
        in_specs=[VM, VM, VM, VM, VM, SM],
        out_specs=[VM] * 3,
        scratch_shapes=[
            pltpu.VMEM((rows, width), F32),
            pltpu.VMEM((3, rows, LANES), F32),
            pltpu.SMEM((r,), jnp.int32),
            pltpu.SemaphoreType.DMA(()),
        ],
        name="near",
    )(everyone, own, hadamard_sample_rows[None], samples, skeleton, ranks)
    picked = gather_cols(picks, 1).reshape(r, width + LANES)
    part, leaf_basis, inverse = pl.pallas_call(
        leaf_kernel,
        out_shape=[shape((r, width), F32), shape((rows, r), BF16), shape((r, r), F32)],
        in_specs=[VM, VM, VM, SM],
        out_specs=[VM] * 3,
        name="leaf",
    )(picked, residue, om, ranks)
    total = reduce_cols(part, 2)
    projected = jnp.dot(inverse, total, precision=HIGH)
    base = 0
    for level in range(1, 4):
        child_base = base
        base = base + (leaf_count >> level - 1)
        pk2, pr2 = swap_siblings([picked, projected], 1 << level - 1, 2 + level)
        last = level == 3
        share, span = r // 8, width // COLS
        out = [shape((share, span), F32)] * 2 if last else [shape((r, width + LANES), F32), shape((r, width), F32)]
        picked, projected = pl.pallas_call(
            functools.partial(merge_kernel, level, child_base, base),
            out_shape=out,
            in_specs=[VM, VM, VM, SM],
            out_specs=[VM] * 2,
            scratch_shapes=[pltpu.VMEM((r, r), F32)] + ([pltpu.VMEM((r, width), F32)] if last else []),
            name=f"merge_{level}",
        )(pk2, pr2, skeleton, ranks)
    return (leaf_basis, picked, projected)


def solution(mesh):
    placed = (
        P(None, ("leaf", "col")),
        P(("leaf", "col")),
        P(("leaf", "col")),
        P(),
        P(("leaf", "col"), None),
        P(),
        P(),
    )
    return jax.shard_map(
        local,
        mesh=mesh,
        in_specs=placed,
        out_specs=(P(("leaf", "col"), None), P("leaf", "col"), P("leaf", "col")),
        check_vma=False,
    )
```

time: 496 us -> 162 us (0.33); the launches traced: 487 us -> 161 us
  waiting for transfers between devices: 207 us -> 0 us
  Pallas kernels: 0 us -> 157 us
  other arithmetic: 101 us -> 0.67 us
  blocking collectives: 62.8 us -> 0 us
  matrix products: 61.6 us -> 2.04 us
  starting transfers between devices: 29.2 us -> 0 us
  between operations: 20.8 us -> 0.73 us
    psum x2 -> x0, waiting for transfers between devices: 185 us -> none  [the longest x1 111 us: local(): projected = lax.psum(jnp.dot(basis.T, own_omega, precision=HIGH), 'col')]
    pallas_call x0 -> x11, Pallas kernels: none -> 157 us  [the longest x3 41.1 us: swap_siblings(): pl.pallas_call(functools.partial(swap_kernel, bit), out_shape=[jax.ShapeD...]
    another operation x21 -> x0, other arithmetic: 92.1 us -> none  [the longest x12 49.6 us: ridge_fit(): factor = jnp.linalg.cholesky(gram + shift * ident)]
    dot_general x28 -> x1, matrix products: 57.5 us -> 2.04 us  [local(): projected = jnp.dot(inverse, total, precision=HIGH)]
    all_gather x2 -> x0, blocking collectives: 39.7 us -> none  [the longest x1 25.1 us: local(): distant_points = lax.all_gather(points, 'col', axis=1, tiled=True)]
    ppermute x9 -> x0, starting transfers between devices: 29.2 us -> none  [swapped(): return lax.ppermute(value, axis, pairs)]
    psum x1 -> x0, blocking collectives: 23.1 us -> none  [local(): picked, spots = lax.psum((part_picked, part_spots), 'col')]
    ppermute x9 -> x0, waiting for transfers between devices: 22.4 us -> none  [swapped(): return lax.ppermute(value, axis, pairs)]
  transfers between devices with their start and end apart: 11 -> 0, of which waited for: 7 -> 0; matrix products, arithmetic and copies ran while one was open for 8% -> 0% of each run, Pallas kernels for 0% -> 0%
where the time goes in v1:
time: 162 us; the launch traced here: 161 us
  Pallas kernels  157 us (97%)
  matrix products  2.04 us (1%)
    pallas_call x3, Pallas kernels, swap_siblings(): pl.pallas_call(functools.partial(swap_kernel, bit), out_shape=[jax.ShapeD...  41.1 us
    pallas_call x2, Pallas kernels, gather_cols(): pl.pallas_call(gather_kernel, out_shape=jax.ShapeDtypeStruct((COLS, *x.sh...  36.6 us
    pallas_call x3, Pallas kernels, local(): pl.pallas_call(functools.partial(merge_kernel, level, child_base, base),...  30.3 us
    pallas_call x1, Pallas kernels, reduce_cols(): pl.pallas_call(reduce_kernel, out_shape=jax.ShapeDtypeStruct(x.shape, x.d...  22.2 us
    pallas_call x1, Pallas kernels, local(): pl.pallas_call(near_kernel, out_shape=[shape((rows, width), F32), shape((...  17.4 us
    pallas_call x1, Pallas kernels, local(): pl.pallas_call(leaf_kernel, out_shape=[shape((r, width), F32), shape((row...  9.25 us

profile of v1, /device:TPU:1, one launch (start us, length us, event | category | flops | bytes accessed | tf_op | source)
XLA Modules:
  0.0 161.0 jit_solution(17426657168306581585)
XLA Ops:
  0.6 0.0 copy-start.2
  0.6 0.0 copy-start.3
  0.7 0.0 copy-start.1
  0.7 0.1 pad.3.clone
  0.7 0.6 copy-done.2
  1.3 0.0 copy-done.3
  1.3 0.0 copy-done.1
  1.4 0.7 maximum_maximum_fusion.x_ref.own_ref
  2.0 20.8 %gather_0.1.all_ref = f32[16,8,512]{2,1,0:T(8,128)} custom-call(f32[8,512]{1,0:T(8,128)} %maximum_maximum_fusion.x_ref.own_ref), custom_call_target="tpu_custom_call" | custom-call | tf_op jit(solution)/shard_map/gather_0/pallas_call | solution.py:132
  22.8 17.4 %near.1 = (f32[512,512]{1,0:T(8,128)}, bf16[512,512]{1,0:T(8,128)(2,1)}, f32[8,640]{1,0:T(8,128)}) custom-call(f32[16,8,512]{2,1,0:T(8,128)} %gather_0.1.all_ref, f32[8,512]{1,0:T(8,128)} %maximum_maximum_fusion.x_ref.own_ref, s32[1,512]{1,0:T(1,128)} %bitcast.10, bf16[512,512]{1,0:T(8,128)(2,1)} %samp_ref.1, s32[60,128]{1,0:T(8,128)} %skel_ref.7, s32[60]{0:T(128)} %rank_ref.9), custom_call_target="tpu_custom_call" | custom-call | tf_op jit(solution)/shard_map/near/pallas_call | solution.py:467
  40.2 15.9 %gather_1.1 = f32[16,8,640]{2,1,0:T(8,128)} custom-call(f32[8,640]{1,0:T(8,128)} %get-tuple-element.21.x_ref), custom_call_target="tpu_custom_call" | custom-call | tf_op jit(solution)/shard_map/gather_1/pallas_call | solution.py:132
  56.0 9.2 %leaf.1 = (f32[128,512]{1,0:T(8,128)}, bf16[512,128]{1,0:T(8,128)(2,1)}, f32[128,128]{1,0:T(8,128)}) custom-call(f32[128,640]{1,0:T(8,128)} %bitcast.6, f32[512,512]{1,0:T(8,128)} %get-tuple-element.22.res_ref, bf16[512,512]{1,0:T(8,128)(2,1)} %get-tuple-element.23.om_ref, s32[60]{0:T(128)} %rank_ref.9), custom_call_target="tpu_custom_call" | custom-call | tf_op jit(solution)/shard_map/leaf/pallas_call | solution.py:481
  65.3 0.0 copy-start
  65.3 22.2 %reduce_2.1 = f32[128,512]{1,0:T(8,128)} custom-call(f32[128,512]{1,0:T(8,128)} %get-tuple-element.26.n_ref), custom_call_target="tpu_custom_call" | custom-call | tf_op jit(solution)/shard_map/reduce_2/pallas_call | solution.py:219
  87.5 0.0 copy-done
  87.5 2.0 %fusion.refs_1_ = f32[128,512]{1,0:T(8,128)} fusion(f32[128,128]{1,0:T(8,128)S(1)} %copy-done, f32[128,512]{1,0:T(8,128)} %reduce_2.1), kind=kOutput, calls=%fused_computation.1 | convolution fusion | flops 100663296 | bytes 589824 | tf_op jit(solution)/shard_map/dot_general | solution.py:489
  89.5 13.2 %swap_3.1 = (f32[2,128,640]{2,1,0:T(8,128)}, f32[2,128,512]{2,1,0:T(8,128)}) custom-call(f32[128,640]{1,0:T(8,128)} %bitcast.7, f32[128,512]{1,0:T(8,128)} %fusion.refs_1_), custom_call_target="tpu_custom_call" | custom-call | tf_op jit(solution)/shard_map/swap_3/pallas_call | solution.py:301
  102.7 10.2 %merge_1.1 = (f32[128,640]{1,0:T(8,128)}, f32[128,512]{1,0:T(8,128)}) custom-call(f32[2,128,640]{2,1,0:T(8,128)} %get-tuple-element.27.pk_ref, f32[2,128,512]{2,1,0:T(8,128)} %get-tuple-element.28.pr_ref, s32[60,128]{1,0:T(8,128)} %skel_ref.7, s32[60]{0:T(128)} %rank_ref.9), custom_call_target="tpu_custom_call" | custom-call | tf_op jit(solution)/shard_map/merge_1/pallas_call | solution.py:498
  112.9 14.7 %swap_4.1 = (f32[2,128,640]{2,1,0:T(8,128)}, f32[2,128,512]{2,1,0:T(8,128)}) custom-call(f32[128,640]{1,0:T(8,128)} %get-tuple-element.29.refs_0_, f32[128,512]{1,0:T(8,128)} %get-tuple-element.30.refs_1_), custom_call_target="tpu_custom_call" | custom-call | tf_op jit(solution)/shard_map/swap_4/pallas_call | solution.py:301
  127.6 10.3 %merge_2.1 = (f32[128,640]{1,0:T(8,128)}, f32[128,512]{1,0:T(8,128)}) custom-call(f32[2,128,640]{2,1,0:T(8,128)} %get-tuple-element.31.pk_ref, f32[2,128,512]{2,1,0:T(8,128)} %get-tuple-element.32.pr_ref, s32[60,128]{1,0:T(8,128)} %skel_ref.7, s32[60]{0:T(128)} %rank_ref.9), custom_call_target="tpu_custom_call" | custom-call | tf_op jit(solution)/shard_map/merge_2/pallas_call | solution.py:498
  137.9 13.2 %swap_5.1 = (f32[2,128,640]{2,1,0:T(8,128)}, f32[2,128,512]{2,1,0:T(8,128)}) custom-call(f32[128,640]{1,0:T(8,128)} %get-tuple-element.33.refs_0_, f32[128,512]{1,0:T(8,128)} %get-tuple-element.34.refs_1_), custom_call_target="tpu_custom_call" | custom-call | tf_op jit(solution)/shard_map/swap_5/pallas_call | solution.py:301
  151.1 9.9 %merge_3.1 = (f32[16,32]{1,0:T(8,128)}, f32[16,32]{1,0:T(8,128)}) custom-call(f32[2,128,640]{2,1,0:T(8,128)} %get-tuple-element.35.pk_ref, f32[2,128,512]{2,1,0:T(8,128)} %get-tuple-element.36.pr_ref, s32[60,128]{1,0:T(8,128)} %skel_ref.7, s32[60]{0:T(128)} %rank_ref.9), custom_call_target="tpu_custom_call" | custom-call | tf_op jit(solution)/shard_map/merge_3/pallas_call | solution.py:498
  (3 shorter events, 0.0 us)
Async XLA Ops:
  0.6 0.7 copy-start.2
  0.6 0.7 copy-start.3
  0.7 0.7 copy-start.1
  65.3 22.2 %copy-start = (f32[128,128]{1,0:T(8,128)S(1)}, f32[128,128]{1,0:T(8,128)}, u32[]{:S(2)}) copy-start(f32[128,128]{1,0:T(8,128)} %get-tuple-element.25) | copy-start | bytes 196612

commit v2 on v0

v2 whole, which is shorter than its diff:
```python
import jax
import jax.numpy as jnp
from jax import lax
from jax.experimental import pallas as pl
from jax.experimental.pallas import tpu as pltpu
from jax.sharding import PartitionSpec as P

MESH = pl.DeviceIdType.MESH
DMA = pltpu.SemaphoreType.DMA
F32 = jnp.float32
BF16 = jnp.bfloat16
VM = pl.BlockSpec(memory_space=pltpu.VMEM)
SM = pl.BlockSpec(memory_space=pltpu.SMEM)
ANY = pl.BlockSpec(memory_space=pl.ANY)

NTOTAL = 1048576
KERNEL_SCALE = 1.0
RIDGE = 0.25
LOG2E = 1.4426950408889634
BITS = NTOTAL.bit_length() - 1
NBITS = 32
PANEL = 16
COLS = 16
ZS = COLS // 2
LANES = 128
LEVELS = 3


def bdot(a, b, ca, cb):
    return lax.dot_general(a, b, (((ca,), (cb,)), ((), ())), preferred_element_type=F32)


def split(x, count):
    pieces = []
    for _ in range(count - 1):
        piece = x.astype(BF16)
        pieces.append(piece)
        x = x - piece.astype(F32)
    return [*pieces, x.astype(BF16)]


def mm(a, b, ca, cb, terms=6):
    count = 3 if terms == 6 else 2
    pa, pb = split(a, count), split(b, count)
    pairs = [(i, j) for i in range(count) for j in range(count) if i + j < count]
    left = jnp.concatenate([pa[i] for i, _ in pairs], ca)
    right = jnp.concatenate([pb[j] for _, j in pairs], cb)
    return bdot(left, right, ca, cb)


def exact(a, b, ca, cb):
    pieces = split(a, 3)
    return bdot(jnp.concatenate(pieces, ca), jnp.concatenate([b] * 3, cb), ca, cb)


def iota(shape, axis):
    return lax.broadcasted_iota(jnp.int32, shape, axis)


def kern(squared_distance):
    return jnp.exp2(squared_distance * (-KERNEL_SCALE * LOG2E))


def spd_inverse(a_ref, hook):
    n = a_ref.shape[0]
    lane = iota((PANEL, n), 1)
    sub = iota((PANEL, n), 0)
    ident = (lane == sub).astype(F32)
    lane_n = iota((n, n), 1)

    def step(b, carry):
        start = pl.multiple_of(b * PANEL, PANEL)
        panel = a_ref[pl.ds(start, PANEL), :]
        rolled = pltpu.roll(panel, lax.rem(n - start, n), 1)
        diag = [jnp.broadcast_to(rolled[:, k : k + 1], (PANEL, n)) for k in range(PANEL)]
        rows = jnp.where(lane < PANEL, ident, rolled)
        for k in range(PANEL):
            inv = 1.0 / diag[k][k : k + 1, :]
            here = sub == k
            factor = diag[k] * inv
            for j in range(k + 1, PANEL):
                own = diag[j][k : k + 1, :]
                diag[j] = jnp.where(here, own * inv, diag[j] - factor * own)
            own = rows[k : k + 1, :]
            rows = jnp.where(here, own * inv, rows - factor * own)
        rows = pltpu.roll(rows, start, 1)
        side = jnp.where(lane < start, -panel, panel)
        side = jnp.where((lane >= start) & (lane < start + PANEL), 0.0, side)
        change = mm(side, rows, 0, 0)
        cleared = jnp.where((lane_n >= start) & (lane_n < start + PANEL), 0.0, a_ref[...])
        a_ref[...] = cleared - change
        a_ref[pl.ds(start, PANEL), :] = rows
        hook(b)
        return carry

    lax.fori_loop(0, n // PANEL, step, 0)


def ridged(gram, rank):
    n = gram.shape[0]
    same = iota((n, n), 0) == iota((n, n), 1)
    trace = jnp.sum(jnp.where(same, gram, 0.0), keepdims=True)
    shift = RIDGE * trace / rank.astype(F32) + 1e-06
    return gram + jnp.where(same, shift, 0.0)


def hss_kernel(
    points_ref, ids_ref, signs_ref, had_ref, samp_hbm, skel_ref, rank_ref,
    basis_ref, top_s, top_o,
    samp, every, om_all, own_b, pick_b, res, raw_ref, part, half, mine, landed, pk, hh, ww, pp, pk3, hh3, ww3,
    samp_sem, g_s, g_r, gp_s, gp_r, p_s, p_r, pp_s, pp_r,
    pair_s, pair_r, rs_s, rs_r, ag_s, ag_r, ap_s, ap_r, ax_s, ax_r, axp_s, axp_r,
    xk_s, xk_r, xkp_s, xkp_r, xh_s, xh_r, xhp_s, xhp_r, xw_s, xw_r, xwp_s, xwp_r,
):
    leaf = lax.axis_index("leaf")
    me = lax.axis_index("col")
    leaves = lax.axis_size("leaf")
    core = lax.rem(me, 2)
    z = me // 2
    partner = me + 1 - 2 * core
    rows = points_ref.shape[1]
    width = had_ref.shape[1]
    r = skel_ref.shape[1]
    count = r // COLS
    sides = [lax.rem(leaf // (1 << lvl), 2) for lvl in range(LEVELS)]
    siblings = [leaf + (1 << lvl) - (2 << lvl) * sides[lvl] for lvl in range(LEVELS)]
    sends = []

    def put(src, dst, send, recv, keep=True, **device):
        copy = pltpu.make_async_remote_copy(
            src_ref=src, dst_ref=dst, send_sem=send, recv_sem=recv, device_id=device, device_id_type=MESH
        )
        if keep:
            sends.append(copy)
        return copy

    def zpeer(off):
        return lax.rem(z + off, ZS)

    fetch = pltpu.make_async_copy(samp_hbm, samp, samp_sem)
    fetch.start()
    barrier = pltpu.get_barrier_semaphore()
    for off in range(1, ZS):
        pl.semaphore_signal(barrier, inc=1, device_id={"col": zpeer(off) * 2 + core}, device_id_type=MESH)
    pl.semaphore_signal(barrier, inc=1, device_id={"col": partner}, device_id_type=MESH)
    for sibling in siblings:
        pl.semaphore_signal(barrier, inc=1, device_id={"leaf": sibling}, device_id_type=MESH)
    every[me, 0:3, :] = points_ref[...]
    every[me, 3:4, :] = ids_ref[...].astype(F32)
    every[me, 4:5, :] = signs_ref[...].astype(F32)
    every[me, 5:8, :] = jnp.zeros((3, rows), F32)
    pl.semaphore_wait(barrier, ZS + LEVELS)

    for off in (1, 7, 2, 6, 3, 5, 4):
        put(every.at[me], every.at[me], g_s.at[off], g_r.at[ZS - off], col=zpeer(off) * 2 + core).start()
    put(every.at[me], every.at[me], gp_s.at[0], gp_r.at[0], col=partner).start()

    bit_row = iota((NBITS, width), 0)
    had = jnp.broadcast_to(had_ref[...], (NBITS, width))
    had_bits = ((had >> jnp.minimum(bit_row, BITS)) & 1).astype(F32) * 0.5
    had_bits = jnp.where(bit_row == BITS, 0.5, jnp.where(bit_row == BITS + 1, 0.25, had_bits))
    had_bits = jnp.where(bit_row > BITS + 1, 0.0, had_bits).astype(BF16)

    def omega4(block):
        shift = iota((NBITS, rows), 0)
        ids = jnp.broadcast_to(block[3:4, :].astype(jnp.int32), (NBITS, rows))
        bits = ((ids >> jnp.minimum(shift, BITS)) & 1).astype(F32)
        bits = jnp.where(shift == BITS, 1.0 - block[4:5, :], bits)
        bits = jnp.where(shift == BITS + 1, 1.0, bits)
        bits = jnp.where(shift > BITS + 1, 0.0, bits).astype(BF16)
        halves = bdot(bits, had_bits, 0, 0)
        return (halves - jnp.round(halves)).astype(BF16)

    ident = (iota((8, LANES), 0) == iota((8, LANES), 1)).astype(BF16)
    own_cols = exact(every[me], ident, 0, 0)
    for axis in range(3):
        own_b[axis] = jnp.broadcast_to(own_cols[:, axis : axis + 1], (rows, LANES))

    my_rows = pl.ds(pl.multiple_of(me * count, count), count)
    entries = jnp.broadcast_to(skel_ref[pl.ds(leaf, 1), :] - me * rows, (rows, r))
    chooser = jnp.where(entries == iota((rows, r), 0), 1.0, 0.0).astype(BF16)
    ww3[...] = bdot(jnp.concatenate([chooser] * 3, 0), jnp.concatenate(split(own_cols, 3), 0), 0, 0)
    spot = ww3[my_rows, :]
    for axis in range(3):
        pick_b[axis] = jnp.broadcast_to(spot[:, axis : axis + 1], (count, LANES))

    def zorder(t):
        return lax.rem(jnp.where(lax.rem(t, 2) == 1, (t + 1) // 2, ZS - t // 2), ZS)

    def tile_of(columns, block):
        tiles = []
        for c in range(rows // LANES):
            d2 = None
            for axis in range(3):
                off = columns[axis] - block[axis : axis + 1, c * LANES : (c + 1) * LANES]
                d2 = off * off if d2 is None else d2 + off * off
            tiles.append(kern(d2).astype(BF16))
        return jnp.concatenate(tiles, 1)

    def scan_blocks(t, acc):
        off = zorder(t)
        there = zpeer(off)
        same = there * 2 + core
        other = there * 2 + 1 - core

        @pl.when(t > 0)
        def _():
            put(every.at[same], every.at[same], g_s.at[off], g_r.at[off], keep=False, col=partner).wait_recv()
            put(every.at[same], every.at[same], gp_s.at[t], gp_r.at[t], keep=False, col=partner).start()

        for slot in (same, other):
            if slot is other:
                put(every.at[slot], every.at[slot], gp_s.at[t], gp_r.at[t], keep=False, col=partner).wait_recv()
            block = every[slot]
            om = omega4(block)
            om_all[slot] = om
            acc = acc + bdot(tile_of([pick_b[axis] for axis in range(3)], block), om, 1, 0)
        return acc

    acc = lax.fori_loop(0, ZS, scan_blocks, jnp.zeros((count, width), F32))
    fetch.wait()
    keep = jnp.where(iota((count, 1), 0) + me * count < rank_ref[leaf], 1.0, 0.0)
    part[...] = bdot(chooser, samp[...], 0, 0)
    pk[0, sides[0], my_rows, 0:width] = (part[my_rows, :] - 0.25 * acc) * keep
    pk[0, sides[0], my_rows, width : width + LANES] = spot

    def pick_rows(slot):
        return pk.at[0, sides[0], pl.ds(pl.multiple_of(slot * count, count), count)]

    for off in (1, 7, 2, 6, 3, 5, 4):
        put(pick_rows(me), pick_rows(me), p_s.at[off], p_r.at[ZS - off], col=zpeer(off) * 2 + core).start()
    put(pick_rows(me), pick_rows(me), pp_s.at[0], pp_r.at[0], col=partner).start()

    res[...] = samp[...].astype(F32)

    def near_step(t, carry):
        off = zorder(t)
        there = zpeer(off)
        same = there * 2 + core

        @pl.when(t > 0)
        def _():
            put(pick_rows(same), pick_rows(same), p_s.at[off], p_r.at[off], keep=False, col=partner).wait_recv()
            put(pick_rows(same), pick_rows(same), pp_s.at[t], pp_r.at[t], keep=False, col=partner).start()

        columns = [own_b[axis] for axis in range(3)]
        tile = jnp.concatenate([tile_of(columns, every[there * 2 + k]) for k in range(2)], 1)
        om = om_all[pl.ds(there * 2, 2)].reshape(2 * rows, width)
        res[...] -= 0.25 * bdot(tile, om, 1, 0)
        return carry

    lax.fori_loop(0, ZS, near_step, 0)

    def finish_relays(t, carry):
        other = zpeer(zorder(t)) * 2 + 1 - core
        put(pick_rows(other), pick_rows(other), pp_s.at[t], pp_r.at[t], keep=False, col=partner).wait_recv()
        return carry

    lax.fori_loop(0, ZS, finish_relays, 0)

    def pieces(buf, level, side, chunks, half_of):
        size = r // 2 // chunks
        return [buf.at[level, side, pl.ds(pl.multiple_of(half_of * (r // 2) + q * size, size), size)] for q in range(chunks)]

    def offer(buf, level, chunks, s, rv):
        for q, piece in enumerate(pieces(buf, level, sides[level], chunks, core)):
            put(piece, piece, s.at[level, q], rv.at[level, q], leaf=siblings[level]).start()

    def relay(buf, level, chunks, s, rv, s2, rv2):
        for q, piece in enumerate(pieces(buf, level, 1 - sides[level], chunks, core)):
            put(piece, piece, s.at[level, q], rv.at[level, q], keep=False, leaf=siblings[level]).wait_recv()
            put(piece, piece, s2.at[level, q], rv2.at[level, q], keep=False, col=partner).start()

    def settle(buf, level, chunks, s2, rv2):
        for q, piece in enumerate(pieces(buf, level, 1 - sides[level], chunks, 1 - core)):
            put(piece, piece, s2.at[level, q], rv2.at[level, q], keep=False, col=partner).wait_recv()

    def drain_relay(buf, level, chunks, s2, rv2):
        for q, piece in enumerate(pieces(buf, level, 1 - sides[level], chunks, core)):
            put(piece, piece, s2.at[level, q], rv2.at[level, q], keep=False, col=partner).wait_send()

    offer(pk, 0, 2, xk_s, xk_r)

    side0 = sides[0]
    picked = pk[0, side0, :, 0:width]
    raw = mm(res[...], picked, 1, 1)
    raw_ref[...] = raw
    om_own = om_all[me]
    part[...] = 0.25 * exact(raw, om_own, 0, 0)
    r2 = r // 2
    own0 = pl.multiple_of(core * r2, r2)
    other0 = pl.multiple_of((1 - core) * r2, r2)
    pair = put(part.at[pl.ds(other0, r2)], half, pair_s, pair_r, col=partner)
    pair.start()
    ww[0, side0] = ridged(mm(picked, picked, 1, 1), rank_ref[leaf])
    scatter = []
    for off in range(1, ZS):
        piece = pl.ds(pl.multiple_of(zpeer(off) * count, count), count)
        scatter.append(put(mine.at[piece], landed.at[off - 1], rs_s.at[off], rs_r.at[off], col=zpeer(off) * 2 + core))

    def leaf_hook(b):
        @pl.when(b == 2)
        def _():
            pair.wait_recv()
            mine[...] = part[pl.ds(own0, r2)] + half[...]
            for copy in scatter:
                copy.start()

        @pl.when(b == 6)
        def _():
            relay(pk, 0, 2, xk_s, xk_r, xkp_s, xkp_r)

    spd_inverse(ww.at[0, side0], leaf_hook)
    offer(ww, 0, 1, xw_s, xw_r)
    basis_ref[...] = mm(raw_ref[...], ww[0, side0], 1, 0).astype(BF16)

    def n_rows(side, half_of, chip):
        return hh.at[0, side, pl.ds(pl.multiple_of(half_of * r2 + chip * count, count), count)]

    total = mine[pl.ds(pl.multiple_of(z * count, count), count)]
    for off in range(1, ZS):
        scatter[off - 1].wait_recv()
        total = total + landed[off - 1]
    hh[0, side0, pl.ds(pl.multiple_of(own0 + z * count, count), count)] = total
    here = n_rows(side0, core, z)
    for off in (1, 7, 2, 6, 3, 5, 4):
        put(here, here, ag_s.at[off], ag_r.at[ZS - off], col=zpeer(off) * 2 + core).start()
    put(here, here, ap_s.at[0], ap_r.at[0], col=partner).start()
    put(here, here, ax_s.at[0], ax_r.at[0], leaf=siblings[0]).start()
    for off in (1, 7, 2, 6, 3, 5, 4):
        got = n_rows(side0, core, zpeer(off))
        put(got, got, ag_s.at[off], ag_r.at[off], keep=False, col=partner).wait_recv()
        put(got, got, ap_s.at[off], ap_r.at[off], col=partner).start()
        put(got, got, ax_s.at[off], ax_r.at[off], leaf=siblings[0]).start()
    relay(ww, 0, 1, xw_s, xw_r, xwp_s, xwp_r)
    for off in (0, 1, 7, 2, 6, 3, 5, 4):
        got = n_rows(1 - side0, core, zpeer(off))
        put(got, got, ax_s.at[off], ax_r.at[off], keep=False, leaf=siblings[0]).wait_recv()
        put(got, got, axp_s.at[off], axp_r.at[off], col=partner).start()
    for off in range(ZS):
        got = n_rows(side0, 1 - core, zpeer(off))
        put(got, got, ap_s.at[off], ap_r.at[off], keep=False, col=partner).wait_recv()
    pp[side0] = mm(ww[0, side0], hh[0, side0], 1, 0)
    settle(pk, 0, 2, xkp_s, xkp_r)
    settle(ww, 0, 1, xwp_s, xwp_r)
    for off in range(ZS):
        got = n_rows(1 - side0, 1 - core, zpeer(off))
        put(got, got, axp_s.at[off], axp_r.at[off], keep=False, col=partner).wait_recv()
    pp[1 - side0] = mm(ww[0, 1 - side0], hh[0, 1 - side0], 1, 0)

    child_base = 0
    base = 0
    sub = iota((r, 1), 0)
    for level in range(1, LEVELS + 1):
        child_base, base = base, base + leaves // (1 << (level - 1))
        node = leaf // (1 << level)
        rank_l = rank_ref[child_base + 2 * node]
        rank_r = rank_ref[child_base + 2 * node + 1]
        rank_p = rank_ref[base + node]
        spots_l = pk[level - 1, 0, :, width : width + LANES]
        spots_r = pk[level - 1, 1, :, width : width + LANES]
        row_r = spots_r.T
        d2 = None
        for axis in range(3):
            off = spots_l[:, axis : axis + 1] - row_r[axis : axis + 1, :]
            d2 = off * off if d2 is None else d2 + off * off
        cross = kern(d2)
        proj_l, proj_r = pp[0], pp[1]
        upper = (pk[level - 1, 0, :, 0:width] - mm(cross, proj_r, 1, 0, 3)) * jnp.where(sub < rank_l, 1.0, 0.0)
        lower = (pk[level - 1, 1, :, 0:width] - mm(cross, proj_l, 0, 0, 3)) * jnp.where(sub < rank_r, 1.0, 0.0)
        cand = jnp.concatenate([upper, lower], 0)
        spots = jnp.concatenate([spots_l, spots_r], 0)
        row = skel_ref[pl.ds(base + node, 1), :]
        chooser = jnp.where(jnp.broadcast_to(row, (2 * r, r)) == iota((2 * r, r), 0), 1.0, 0.0).astype(BF16)
        three = split(jnp.concatenate([cand, spots], 1), 3)
        chosen = bdot(jnp.concatenate([chooser] * 3, 0), jnp.concatenate(three, 0), 0, 0)
        picked = chosen[:, 0:width] * jnp.where(sub < rank_p, 1.0, 0.0)
        last = level == LEVELS
        if not last:
            side = sides[level]
            pk[level, side, :, 0:width] = picked
            pk[level, side, :, width : width + LANES] = chosen[:, width : width + LANES]
            offer(pk, level, 2, xk_s, xk_r)
        else:
            pk3[...] = picked
        raw = mm(cand, picked, 1, 1, 3)
        back = mm(raw, jnp.concatenate([proj_l, proj_r], 0), 0, 0)
        if not last:
            hh[level, side] = back
            offer(hh, level, 2, xh_s, xh_r)
        else:
            hh3[...] = back
        gram = ridged(mm(picked, picked, 1, 1, 3), rank_p)
        if not last:
            ww[level, side] = gram

            def hook(b, level=level):
                @pl.when(b == 4)
                def _():
                    relay(pk, level, 2, xk_s, xk_r, xkp_s, xkp_r)

            spd_inverse(ww.at[level, side], hook)
            offer(ww, level, 1, xw_s, xw_r)
            pp[side] = mm(ww[level, side], hh[level, side], 1, 0)
            relay(hh, level, 2, xh_s, xh_r, xhp_s, xhp_r)
            relay(ww, level, 1, xw_s, xw_r, xwp_s, xwp_r)
            settle(pk, level, 2, xkp_s, xkp_r)
            settle(hh, level, 2, xhp_s, xhp_r)
            settle(ww, level, 1, xwp_s, xwp_r)
            pp[1 - side] = mm(ww[level, 1 - side], hh[level, 1 - side], 1, 0)
        else:
            ww3[...] = gram
            spd_inverse(ww3, lambda b: None)
            share, span = top_s.shape
            turn = lax.rem(width - me * span, width)
            mine_rows = pl.ds(pl.multiple_of(lax.rem(leaf, 8) * share, share), share)
            top_s[...] = pltpu.roll(pk3[mine_rows, :], turn, 1)[:, 0:span]
            top_o[...] = pltpu.roll(mm(ww3[mine_rows, :], hh3[...], 1, 0), turn, 1)[:, 0:span]

    for copy in sends:
        copy.wait_send()
    for level in range(LEVELS):
        drain_relay(pk, level, 2, xkp_s, xkp_r)
        drain_relay(ww, level, 1, xwp_s, xwp_r)
        if level > 0:
            drain_relay(hh, level, 2, xhp_s, xhp_r)

    def drain(t, carry):
        same = zpeer(zorder(t)) * 2 + core
        put(every.at[same], every.at[same], gp_s.at[t], gp_r.at[t], keep=False, col=partner).wait_send()
        put(pick_rows(same), pick_rows(same), pp_s.at[t], pp_r.at[t], keep=False, col=partner).wait_send()
        return carry

    lax.fori_loop(1, ZS, drain, 0)


def local(points, point_ids, signs, hadamard_sample_rows, samples, skeleton, ranks):
    rows = points.shape[1]
    width = samples.shape[1]
    r = skeleton.shape[1]
    count = r // COLS
    shape = jax.ShapeDtypeStruct
    fetched = pltpu.VMEM
    sems = [DMA(()), *[DMA((ZS,))] * 8, DMA(()), DMA(()), *[DMA((ZS,))] * 10, *[DMA((LEVELS, 2))] * 12]
    return pl.pallas_call(
        hss_kernel,
        out_shape=[
            shape((rows, r), BF16),
            shape((r // 8, width // COLS), F32),
            shape((r // 8, width // COLS), F32),
        ],
        in_specs=[VM, VM, VM, VM, ANY, VM, SM],
        out_specs=[VM] * 3,
        scratch_shapes=[
            fetched((rows, width), BF16),
            fetched((COLS, 8, rows), F32),
            fetched((COLS, rows, width), BF16),
            fetched((3, rows, LANES), F32),
            fetched((3, count, LANES), F32),
            fetched((rows, width), F32),
            fetched((rows, r), F32),
            fetched((r, width), F32),
            fetched((r // 2, width), F32),
            fetched((r // 2, width), F32),
            fetched((ZS - 1, count, width), F32),
            fetched((LEVELS, 2, r, width + LANES), F32),
            fetched((LEVELS, 2, r, width), F32),
            fetched((LEVELS, 2, r, r), F32),
            fetched((2, r, width), F32),
            fetched((r, width), F32),
            fetched((r, width), F32),
            fetched((r, r), F32),
            *sems,
        ],
        compiler_params=pltpu.CompilerParams(collective_id=0, has_side_effects=True),
        name="hss",
    )(points, point_ids[None], signs[None], hadamard_sample_rows[None], samples, skeleton, ranks)


def solution(mesh):
    placed = (
        P(None, ("leaf", "col")),
        P(("leaf", "col")),
        P(("leaf", "col")),
        P(),
        P(("leaf", "col"), None),
        P(),
        P(),
    )
    return jax.shard_map(
        local,
        mesh=mesh,
        in_specs=placed,
        out_specs=(P(("leaf", "col"), None), P("leaf", "col"), P("leaf", "col")),
        check_vma=False,
    )
```

time: 496 us -> 95.6 us (0.19); the launches traced: 487 us -> 95.3 us
  waiting for transfers between devices: 207 us -> 0 us
  other arithmetic: 101 us -> 0 us
  Pallas kernels: 0 us -> 91.8 us
  blocking collectives: 62.8 us -> 0 us
  matrix products: 61.6 us -> 0 us
  starting transfers between devices: 29.2 us -> 0 us
  between operations: 20.8 us -> 0.65 us
    psum x2 -> x0, waiting for transfers between devices: 185 us -> none  [the longest x1 111 us: local(): projected = lax.psum(jnp.dot(basis.T, own_omega, precision=HIGH), 'col')]
    another operation x21 -> x0, other arithmetic: 92.1 us -> none  [the longest x12 49.6 us: ridge_fit(): factor = jnp.linalg.cholesky(gram + shift * ident)]
    pallas_call x0 -> x1, Pallas kernels: none -> 91.8 us  [local(): pl.pallas_call(hss_kernel, out_shape=[shape((rows, r), BF16), shape((r //...]
    dot_general x28 -> x0, matrix products: 57.5 us -> none  [the longest x2 33.3 us: omega_rows(): counted = jnp.dot(row_bits, col_bits, precision=HIGH)]
    all_gather x2 -> x0, blocking collectives: 39.7 us -> none  [the longest x1 25.1 us: local(): distant_points = lax.all_gather(points, 'col', axis=1, tiled=True)]
    ppermute x9 -> x0, starting transfers between devices: 29.2 us -> none  [swapped(): return lax.ppermute(value, axis, pairs)]
    psum x1 -> x0, blocking collectives: 23.1 us -> none  [local(): picked, spots = lax.psum((part_picked, part_spots), 'col')]
    ppermute x9 -> x0, waiting for transfers between devices: 22.4 us -> none  [swapped(): return lax.ppermute(value, axis, pairs)]
  transfers between devices with their start and end apart: 11 -> 0, of which waited for: 7 -> 0; matrix products, arithmetic and copies ran while one was open for 8% -> 0% of each run, Pallas kernels for 0% -> 0%
where the time goes in v2:
time: 95.6 us; the launch traced here: 95.3 us
  Pallas kernels  91.8 us (96%)
  local copies, waits for them, and re-layouts  2.88 us (3%)
    pallas_call x1, Pallas kernels, local(): pl.pallas_call(hss_kernel, out_shape=[shape((rows, r), BF16), shape((r //...  91.8 us
    unnamed x7, local copies, waits for them, and re-layouts  2.88 us

profile of v2, /device:TPU:1, one launch (start us, length us, event | category | flops | bytes accessed | tf_op | source)
XLA Modules:
  0.0 95.3 jit_solution(5413985038445857806)
XLA Ops:
  0.6 91.8 %hss.1 = (bf16[512,128]{1,0:T(8,128)(2,1)}, f32[16,32]{1,0:T(8,128)}, f32[16,32]{1,0:T(8,128)}) custom-call(f32[3,512]{1,0:T(4,128)} %points_ref.1, s32[1,512]{1,0:T(1,128)} %bitcast.3, s32[1,512]{1,0:T(1,128)} %bitcast.4, s32[1,512]{1,0:T(1,128)} %bitcast.5, bf16[512,512]{1,0:T(8,128)(2,1)} %samp_hbm.1, s32[60,128]{1,0:T(8,128)} %skel_ref.1, s32[60]{0:T(128)} %rank_ref.1), custom_call_target="tpu_custom_call" | custom-call | tf_op jit(solution)/shard_map/hss/pallas_call | solution.py:445
  92.5 0.0 copy-start.1
  92.5 1.6 %copy.13 = bf16[512,128]{1,0:T(8,128)(2,1)} copy(bf16[512,128]{1,0:T(8,128)(2,1)} %get-tuple-element.6) | data formatting | bytes 262144
  94.0 0.0 copy-done.1
  94.0 0.0 copy-start
  94.0 0.6 copy.14
  94.6 0.1 copy-done
  94.7 0.6 copy.15
Async XLA Ops:
  92.5 1.6 %copy-start.1 = (f32[16,32]{1,0:T(8,128)S(1)}, f32[16,32]{1,0:T(8,128)}, u32[]{:S(2)}) copy-start(f32[16,32]{1,0:T(8,128)} %get-tuple-element.7) | copy-start | bytes 6148
  94.0 0.7 copy-start

commit v3 on v2

--- a/solution.py
+++ b/solution.py
@@ -107,10 +107,10 @@
 def hss_kernel(
     points_ref, ids_ref, signs_ref, had_ref, samp_hbm, skel_ref, rank_ref,
     basis_ref, top_s, top_o,
-    samp, every, om_all, own_b, pick_b, res, raw_ref, part, half, mine, landed, pk, hh, ww, pp, pk3, hh3, ww3,
+    samp, every, om_all, own_b, pick_b, res, raw_ref, part, half, mine, landed, spk, pk, sp, hh, ww, pp, pk3, hh3, ww3,
     samp_sem, g_s, g_r, gp_s, gp_r, p_s, p_r, pp_s, pp_r,
     pair_s, pair_r, rs_s, rs_r, ag_s, ag_r, ap_s, ap_r, ax_s, ax_r, axp_s, axp_r,
-    xk_s, xk_r, xkp_s, xkp_r, xh_s, xh_r, xhp_s, xhp_r, xw_s, xw_r, xwp_s, xwp_r,
+    xs_s, xs_r, xk_s, xk_r, xkp_s, xkp_r, xh_s, xh_r, xhp_s, xhp_r, xw_s, xw_r, xwp_s, xwp_r,
 ):
     leaf = lax.axis_index("leaf")
     me = lax.axis_index("col")
@@ -149,17 +149,41 @@
     every[me, 3:4, :] = ids_ref[...].astype(F32)
     every[me, 4:5, :] = signs_ref[...].astype(F32)
     every[me, 5:8, :] = jnp.zeros((3, rows), F32)
-    pl.semaphore_wait(barrier, ZS + LEVELS)
-
-    for off in (1, 7, 2, 6, 3, 5, 4):
-        put(every.at[me], every.at[me], g_s.at[off], g_r.at[ZS - off], col=zpeer(off) * 2 + core).start()
-    put(every.at[me], every.at[me], gp_s.at[0], gp_r.at[0], col=partner).start()
-
+
+    my_rows = pl.ds(pl.multiple_of(me * count, count), count)
+    entry = skel_ref[pl.ds(leaf, 1), :]
+
+    def chooser_of(slot):
+        return jnp.where(
+            jnp.broadcast_to(entry - slot * rows, (rows, r)) == iota((rows, r), 0), 1.0, 0.0
+        ).astype(BF16)
+
+    fetch.wait()
+    part[...] = bdot(chooser_of(me), samp[...], 0, 0)
+    spk[my_rows, :] = part[my_rows, :]
+
+    ident = (iota((8, LANES), 0) == iota((8, LANES), 1)).astype(BF16)
+    own_cols = exact(every[me], ident, 0, 0)
+    for axis in range(3):
+        own_b[axis] = jnp.broadcast_to(own_cols[:, axis : axis + 1], (rows, LANES))
     bit_row = iota((NBITS, width), 0)
     had = jnp.broadcast_to(had_ref[...], (NBITS, width))
     had_bits = ((had >> jnp.minimum(bit_row, BITS)) & 1).astype(F32) * 0.5
     had_bits = jnp.where(bit_row == BITS, 0.5, jnp.where(bit_row == BITS + 1, 0.25, had_bits))
     had_bits = jnp.where(bit_row > BITS + 1, 0.0, had_bits).astype(BF16)
+    res[...] = samp[...].astype(F32)
+    pl.semaphore_wait(barrier, ZS + LEVELS)
+
+    def pick_rows(slot):
+        return spk.at[pl.ds(pl.multiple_of(slot * count, count), count)]
+
+    order = (1, 7, 2, 6, 3, 5, 4)
+    for off in order:
+        put(every.at[me], every.at[me], g_s.at[off], g_r.at[ZS - off], col=zpeer(off) * 2 + core).start()
+    put(every.at[me], every.at[me], gp_s.at[0], gp_r.at[0], col=partner).start()
+    for off in order:
+        put(pick_rows(me), pick_rows(me), p_s.at[off], p_r.at[ZS - off], col=zpeer(off) * 2 + core).start()
+    put(pick_rows(me), pick_rows(me), pp_s.at[0], pp_r.at[0], col=partner).start()
 
     def omega4(block):
         shift = iota((NBITS, rows), 0)
@@ -171,19 +195,6 @@
         halves = bdot(bits, had_bits, 0, 0)
         return (halves - jnp.round(halves)).astype(BF16)
 
-    ident = (iota((8, LANES), 0) == iota((8, LANES), 1)).astype(BF16)
-    own_cols = exact(every[me], ident, 0, 0)
-    for axis in range(3):
-        own_b[axis] = jnp.broadcast_to(own_cols[:, axis : axis + 1], (rows, LANES))
-
-    my_rows = pl.ds(pl.multiple_of(me * count, count), count)
-    entries = jnp.broadcast_to(skel_ref[pl.ds(leaf, 1), :] - me * rows, (rows, r))
-    chooser = jnp.where(entries == iota((rows, r), 0), 1.0, 0.0).astype(BF16)
-    ww3[...] = bdot(jnp.concatenate([chooser] * 3, 0), jnp.concatenate(split(own_cols, 3), 0), 0, 0)
-    spot = ww3[my_rows, :]
-    for axis in range(3):
-        pick_b[axis] = jnp.broadcast_to(spot[:, axis : axis + 1], (count, LANES))
-
     def zorder(t):
         return lax.rem(jnp.where(lax.rem(t, 2) == 1, (t + 1) // 2, ZS - t // 2), ZS)
 
@@ -197,7 +208,7 @@
             tiles.append(kern(d2).astype(BF16))
         return jnp.concatenate(tiles, 1)
 
-    def scan_blocks(t, acc):
+    def near_step(t, spots):
         off = zorder(t)
         there = zpeer(off)
         same = there * 2 + core
@@ -208,55 +219,46 @@
             put(every.at[same], every.at[same], g_s.at[off], g_r.at[off], keep=False, col=partner).wait_recv()
             put(every.at[same], every.at[same], gp_s.at[t], gp_r.at[t], keep=False, col=partner).start()
 
-        for slot in (same, other):
-            if slot is other:
-                put(every.at[slot], every.at[slot], gp_s.at[t], gp_r.at[t], keep=False, col=partner).wait_recv()
-            block = every[slot]
+        put(every.at[other], every.at[other], gp_s.at[t], gp_r.at[t], keep=False, col=partner).wait_recv()
+        columns = [own_b[axis] for axis in range(3)]
+        tiles, omegas = [], []
+        for k in range(2):
+            block = every[there * 2 + k]
+            spots = spots + exact(block, chooser_of(there * 2 + k), 1, 0)
             om = omega4(block)
-            om_all[slot] = om
-            acc = acc + bdot(tile_of([pick_b[axis] for axis in range(3)], block), om, 1, 0)
-        return acc
-
-    acc = lax.fori_loop(0, ZS, scan_blocks, jnp.zeros((count, width), F32))
-    fetch.wait()
-    keep = jnp.where(iota((count, 1), 0) + me * count < rank_ref[leaf], 1.0, 0.0)
-    part[...] = bdot(chooser, samp[...], 0, 0)
-    pk[0, sides[0], my_rows, 0:width] = (part[my_rows, :] - 0.25 * acc) * keep
-    pk[0, sides[0], my_rows, width : width + LANES] = spot
-
-    def pick_rows(slot):
-        return pk.at[0, sides[0], pl.ds(pl.multiple_of(slot * count, count), count)]
-
-    for off in (1, 7, 2, 6, 3, 5, 4):
-        put(pick_rows(me), pick_rows(me), p_s.at[off], p_r.at[ZS - off], col=zpeer(off) * 2 + core).start()
-    put(pick_rows(me), pick_rows(me), pp_s.at[0], pp_r.at[0], col=partner).start()
-
-    res[...] = samp[...].astype(F32)
-
-    def near_step(t, carry):
-        off = zorder(t)
-        there = zpeer(off)
-        same = there * 2 + core
+            om_all[there * 2 + k] = om
+            omegas.append(om)
+            tiles.append(tile_of(columns, block))
+        res[...] -= 0.25 * bdot(jnp.concatenate(tiles, 1), jnp.concatenate(omegas, 0), 1, 0)
 
         @pl.when(t > 0)
         def _():
             put(pick_rows(same), pick_rows(same), p_s.at[off], p_r.at[off], keep=False, col=partner).wait_recv()
             put(pick_rows(same), pick_rows(same), pp_s.at[t], pp_r.at[t], keep=False, col=partner).start()
 
-        columns = [own_b[axis] for axis in range(3)]
+        return spots
+
+    spots = lax.fori_loop(0, ZS, near_step, jnp.zeros((8, r), F32))
+    sp[0, sides[0]] = spots
+    put(sp.at[0, sides[0]], sp.at[0, sides[0]], xs_s.at[0], xs_r.at[0], leaf=siblings[0]).start()
+
+    spot_cols = exact(spots, ident, 0, 0)
+    for axis in range(3):
+        pick_b[axis] = jnp.broadcast_to(spot_cols[:, axis : axis + 1], (r, LANES))
+    part[...] = jnp.zeros((r, width), F32)
+
+    def pick_step(t, carry):
+        there = zpeer(zorder(t))
+        other = there * 2 + 1 - core
+        columns = [pick_b[axis] for axis in range(3)]
         tile = jnp.concatenate([tile_of(columns, every[there * 2 + k]) for k in range(2)], 1)
-        om = om_all[pl.ds(there * 2, 2)].reshape(2 * rows, width)
-        res[...] -= 0.25 * bdot(tile, om, 1, 0)
-        return carry
-
-    lax.fori_loop(0, ZS, near_step, 0)
-
-    def finish_relays(t, carry):
-        other = zpeer(zorder(t)) * 2 + 1 - core
+        part[...] += bdot(tile, om_all[pl.ds(there * 2, 2)].reshape(2 * rows, width), 1, 0)
         put(pick_rows(other), pick_rows(other), pp_s.at[t], pp_r.at[t], keep=False, col=partner).wait_recv()
         return carry
 
-    lax.fori_loop(0, ZS, finish_relays, 0)
+    lax.fori_loop(0, ZS, pick_step, 0)
+    sub = iota((r, 1), 0)
+    pk[0, sides[0]] = (spk[...] - 0.25 * part[...]) * jnp.where(sub < rank_ref[leaf], 1.0, 0.0)
 
     def pieces(buf, level, side, chunks, half_of):
         size = r // 2 // chunks
@@ -275,6 +277,10 @@
         for q, piece in enumerate(pieces(buf, level, 1 - sides[level], chunks, 1 - core)):
             put(piece, piece, s2.at[level, q], rv2.at[level, q], keep=False, col=partner).wait_recv()
 
+    def hear(level):
+        got = sp.at[level, 1 - sides[level]]
+        put(got, got, xs_s.at[level], xs_r.at[level], keep=False, leaf=siblings[level]).wait_recv()
+
     def drain_relay(buf, level, chunks, s2, rv2):
         for q, piece in enumerate(pieces(buf, level, 1 - sides[level], chunks, core)):
             put(piece, piece, s2.at[level, q], rv2.at[level, q], keep=False, col=partner).wait_send()
@@ -282,7 +288,7 @@
     offer(pk, 0, 2, xk_s, xk_r)
 
     side0 = sides[0]
-    picked = pk[0, side0, :, 0:width]
+    picked = pk[0, side0]
     raw = mm(res[...], picked, 1, 1)
     raw_ref[...] = raw
     om_own = om_all[me]
@@ -342,6 +348,7 @@
         put(got, got, ap_s.at[off], ap_r.at[off], keep=False, col=partner).wait_recv()
     pp[side0] = mm(ww[0, side0], hh[0, side0], 1, 0)
     settle(pk, 0, 2, xkp_s, xkp_r)
+    hear(0)
     settle(ww, 0, 1, xwp_s, xwp_r)
     for off in range(ZS):
         got = n_rows(1 - side0, 1 - core, zpeer(off))
@@ -350,37 +357,36 @@
 
     child_base = 0
     base = 0
-    sub = iota((r, 1), 0)
     for level in range(1, LEVELS + 1):
         child_base, base = base, base + leaves // (1 << (level - 1))
         node = leaf // (1 << level)
         rank_l = rank_ref[child_base + 2 * node]
         rank_r = rank_ref[child_base + 2 * node + 1]
         rank_p = rank_ref[base + node]
-        spots_l = pk[level - 1, 0, :, width : width + LANES]
-        spots_r = pk[level - 1, 1, :, width : width + LANES]
-        row_r = spots_r.T
+        spots_l = exact(sp[level - 1, 0], ident, 0, 0)
+        row_r = sp[level - 1, 1]
         d2 = None
         for axis in range(3):
             off = spots_l[:, axis : axis + 1] - row_r[axis : axis + 1, :]
             d2 = off * off if d2 is None else d2 + off * off
         cross = kern(d2)
         proj_l, proj_r = pp[0], pp[1]
-        upper = (pk[level - 1, 0, :, 0:width] - mm(cross, proj_r, 1, 0, 3)) * jnp.where(sub < rank_l, 1.0, 0.0)
-        lower = (pk[level - 1, 1, :, 0:width] - mm(cross, proj_l, 0, 0, 3)) * jnp.where(sub < rank_r, 1.0, 0.0)
+        upper = (pk[level - 1, 0] - mm(cross, proj_r, 1, 0, 3)) * jnp.where(sub < rank_l, 1.0, 0.0)
+        lower = (pk[level - 1, 1] - mm(cross, proj_l, 0, 0, 3)) * jnp.where(sub < rank_r, 1.0, 0.0)
         cand = jnp.concatenate([upper, lower], 0)
-        spots = jnp.concatenate([spots_l, spots_r], 0)
+        spots = jnp.concatenate([sp[level - 1, 0], row_r], 1)
         row = skel_ref[pl.ds(base + node, 1), :]
         chooser = jnp.where(jnp.broadcast_to(row, (2 * r, r)) == iota((2 * r, r), 0), 1.0, 0.0).astype(BF16)
-        three = split(jnp.concatenate([cand, spots], 1), 3)
+        three = split(cand, 3)
         chosen = bdot(jnp.concatenate([chooser] * 3, 0), jnp.concatenate(three, 0), 0, 0)
-        picked = chosen[:, 0:width] * jnp.where(sub < rank_p, 1.0, 0.0)
+        picked = chosen * jnp.where(sub < rank_p, 1.0, 0.0)
         last = level == LEVELS
         if not last:
             side = sides[level]
-            pk[level, side, :, 0:width] = picked
-            pk[level, side, :, width : width + LANES] = chosen[:, width : width + LANES]
+            pk[level, side] = picked
+            sp[level, side] = exact(spots, chooser, 1, 0)
             offer(pk, level, 2, xk_s, xk_r)
+            put(sp.at[level, side], sp.at[level, side], xs_s.at[level], xs_r.at[level], leaf=siblings[level]).start()
         else:
             pk3[...] = picked
         raw = mm(cand, picked, 1, 1, 3)
@@ -405,6 +411,7 @@
             relay(hh, level, 2, xh_s, xh_r, xhp_s, xhp_r)
             relay(ww, level, 1, xw_s, xw_r, xwp_s, xwp_r)
             settle(pk, level, 2, xkp_s, xkp_r)
+            hear(level)
             settle(hh, level, 2, xhp_s, xhp_r)
             settle(ww, level, 1, xwp_s, xwp_r)
             pp[1 - side] = mm(ww[level, 1 - side], hh[level, 1 - side], 1, 0)
@@ -441,7 +448,7 @@
     count = r // COLS
     shape = jax.ShapeDtypeStruct
     fetched = pltpu.VMEM
-    sems = [DMA(()), *[DMA((ZS,))] * 8, DMA(()), DMA(()), *[DMA((ZS,))] * 10, *[DMA((LEVELS, 2))] * 12]
+    sems = [DMA(()), *[DMA((ZS,))] * 8, DMA(()), DMA(()), *[DMA((ZS,))] * 10, *[DMA((LEVELS,))] * 2, *[DMA((LEVELS, 2))] * 12]
     return pl.pallas_call(
         hss_kernel,
         out_shape=[
@@ -456,14 +463,16 @@
             fetched((COLS, 8, rows), F32),
             fetched((COLS, rows, width), BF16),
             fetched((3, rows, LANES), F32),
-            fetched((3, count, LANES), F32),
+            fetched((3, r, LANES), F32),
             fetched((rows, width), F32),
             fetched((rows, r), F32),
             fetched((r, width), F32),
             fetched((r // 2, width), F32),
             fetched((r // 2, width), F32),
             fetched((ZS - 1, count, width), F32),
-            fetched((LEVELS, 2, r, width + LANES), F32),
+            fetched((r, width), F32),
+            fetched((LEVELS, 2, r, width), F32),
+            fetched((LEVELS, 2, 8, r), F32),
             fetched((LEVELS, 2, r, width), F32),
             fetched((LEVELS, 2, r, r), F32),
             fetched((2, r, width), F32),

time: 95.6 us -> 95 us (level)
  no operation moved by 1% of the time
where the time goes in v3:
time: 95 us; the launch traced here: 94.7 us
  Pallas kernels  91.1 us (96%)
  local copies, waits for them, and re-layouts  2.88 us (3%)
    pallas_call x1, Pallas kernels, local(): pl.pallas_call(hss_kernel, out_shape=[shape((rows, r), BF16), shape((r //...  91.1 us
    unnamed x7, local copies, waits for them, and re-layouts  2.88 us

profile of v3, /device:TPU:1, one launch (start us, length us, event | category | flops | bytes accessed | tf_op | source)
XLA Modules:
  0.0 94.7 jit_solution(1740412561883355046)
XLA Ops:
  0.6 91.1 %hss.1 = (bf16[512,128]{1,0:T(8,128)(2,1)}, f32[16,32]{1,0:T(8,128)}, f32[16,32]{1,0:T(8,128)}) custom-call(f32[3,512]{1,0:T(4,128)} %points_ref.1, s32[1,512]{1,0:T(1,128)} %bitcast.3, s32[1,512]{1,0:T(1,128)} %bitcast.4, s32[1,512]{1,0:T(1,128)} %bitcast.5, bf16[512,512]{1,0:T(8,128)(2,1)} %samp_hbm.1, s32[60,128]{1,0:T(8,128)} %skel_ref.1, s32[60]{0:T(128)} %rank_ref.1), custom_call_target="tpu_custom_call" | custom-call | tf_op jit(solution)/shard_map/hss/pallas_call | solution.py:452
  91.8 0.0 copy-start.1
  91.8 1.6 %copy.13 = bf16[512,128]{1,0:T(8,128)(2,1)} copy(bf16[512,128]{1,0:T(8,128)(2,1)} %get-tuple-element.6) | data formatting | bytes 262144
  93.4 0.0 copy-done.1
  93.4 0.0 copy-start
  93.4 0.6 copy.14
  94.0 0.1 copy-done
  94.1 0.6 copy.15
Async XLA Ops:
  91.8 1.6 %copy-start.1 = (f32[16,32]{1,0:T(8,128)S(1)}, f32[16,32]{1,0:T(8,128)}, u32[]{:S(2)}) copy-start(f32[16,32]{1,0:T(8,128)} %get-tuple-element.7) | copy-start | bytes 6148
  93.4 0.7 copy-start

commit v4 on v3

--- a/solution.py
+++ b/solution.py
@@ -148,7 +148,7 @@
     every[me, 0:3, :] = points_ref[...]
     every[me, 3:4, :] = ids_ref[...].astype(F32)
     every[me, 4:5, :] = signs_ref[...].astype(F32)
-    every[me, 5:8, :] = jnp.zeros((3, rows), F32)
+    every[:, 5:8, :] = jnp.zeros((COLS, 3, rows), F32)
 
     my_rows = pl.ds(pl.multiple_of(me * count, count), count)
     entry = skel_ref[pl.ds(leaf, 1), :]
@@ -177,10 +177,13 @@
     def pick_rows(slot):
         return spk.at[pl.ds(pl.multiple_of(slot * count, count), count)]
 
+    def block_of(slot):
+        return every.at[slot, pl.ds(0, 5)]
+
     order = (1, 7, 2, 6, 3, 5, 4)
     for off in order:
-        put(every.at[me], every.at[me], g_s.at[off], g_r.at[ZS - off], col=zpeer(off) * 2 + core).start()
-    put(every.at[me], every.at[me], gp_s.at[0], gp_r.at[0], col=partner).start()
+        put(block_of(me), block_of(me), g_s.at[off], g_r.at[ZS - off], col=zpeer(off) * 2 + core).start()
+    put(block_of(me), block_of(me), gp_s.at[0], gp_r.at[0], col=partner).start()
     for off in order:
         put(pick_rows(me), pick_rows(me), p_s.at[off], p_r.at[ZS - off], col=zpeer(off) * 2 + core).start()
     put(pick_rows(me), pick_rows(me), pp_s.at[0], pp_r.at[0], col=partner).start()
@@ -216,10 +219,10 @@
 
         @pl.when(t > 0)
         def _():
-            put(every.at[same], every.at[same], g_s.at[off], g_r.at[off], keep=False, col=partner).wait_recv()
-            put(every.at[same], every.at[same], gp_s.at[t], gp_r.at[t], keep=False, col=partner).start()
-
-        put(every.at[other], every.at[other], gp_s.at[t], gp_r.at[t], keep=False, col=partner).wait_recv()
+            put(block_of(same), block_of(same), g_s.at[off], g_r.at[off], keep=False, col=partner).wait_recv()
+            put(block_of(same), block_of(same), gp_s.at[t], gp_r.at[t], keep=False, col=partner).start()
+
+        put(block_of(other), block_of(other), gp_s.at[t], gp_r.at[t], keep=False, col=partner).wait_recv()
         columns = [own_b[axis] for axis in range(3)]
         tiles, omegas = [], []
         for k in range(2):
@@ -231,11 +234,6 @@
             tiles.append(tile_of(columns, block))
         res[...] -= 0.25 * bdot(jnp.concatenate(tiles, 1), jnp.concatenate(omegas, 0), 1, 0)
 
-        @pl.when(t > 0)
-        def _():
-            put(pick_rows(same), pick_rows(same), p_s.at[off], p_r.at[off], keep=False, col=partner).wait_recv()
-            put(pick_rows(same), pick_rows(same), pp_s.at[t], pp_r.at[t], keep=False, col=partner).start()
-
         return spots
 
     spots = lax.fori_loop(0, ZS, near_step, jnp.zeros((8, r), F32))
@@ -247,16 +245,30 @@
         pick_b[axis] = jnp.broadcast_to(spot_cols[:, axis : axis + 1], (r, LANES))
     part[...] = jnp.zeros((r, width), F32)
 
+    def pick_relay(t, carry):
+        off = zorder(t)
+        same = zpeer(off) * 2 + core
+        put(pick_rows(same), pick_rows(same), p_s.at[off], p_r.at[off], keep=False, col=partner).wait_recv()
+        put(pick_rows(same), pick_rows(same), pp_s.at[t], pp_r.at[t], keep=False, col=partner).start()
+        return carry
+
+    lax.fori_loop(1, ZS, pick_relay, 0)
+
     def pick_step(t, carry):
         there = zpeer(zorder(t))
-        other = there * 2 + 1 - core
         columns = [pick_b[axis] for axis in range(3)]
         tile = jnp.concatenate([tile_of(columns, every[there * 2 + k]) for k in range(2)], 1)
         part[...] += bdot(tile, om_all[pl.ds(there * 2, 2)].reshape(2 * rows, width), 1, 0)
+        return carry
+
+    lax.fori_loop(0, ZS, pick_step, 0)
+
+    def pick_settle(t, carry):
+        other = zpeer(zorder(t)) * 2 + 1 - core
         put(pick_rows(other), pick_rows(other), pp_s.at[t], pp_r.at[t], keep=False, col=partner).wait_recv()
         return carry
 
-    lax.fori_loop(0, ZS, pick_step, 0)
+    lax.fori_loop(0, ZS, pick_settle, 0)
     sub = iota((r, 1), 0)
     pk[0, sides[0]] = (spk[...] - 0.25 * part[...]) * jnp.where(sub < rank_ref[leaf], 1.0, 0.0)
 
@@ -434,7 +446,7 @@
 
     def drain(t, carry):
         same = zpeer(zorder(t)) * 2 + core
-        put(every.at[same], every.at[same], gp_s.at[t], gp_r.at[t], keep=False, col=partner).wait_send()
+        put(block_of(same), block_of(same), gp_s.at[t], gp_r.at[t], keep=False, col=partner).wait_send()
         put(pick_rows(same), pick_rows(same), pp_s.at[t], pp_r.at[t], keep=False, col=partner).wait_send()
         return carry
 

time: 95 us -> 95.3 us (level)
  no operation moved by 1% of the time
where the time goes in v4:
time: 95.3 us; the launch traced here: 95 us
  Pallas kernels  91.5 us (96%)
  local copies, waits for them, and re-layouts  2.88 us (3%)
    pallas_call x1, Pallas kernels, local(): pl.pallas_call(hss_kernel, out_shape=[shape((rows, r), BF16), shape((r //...  91.5 us
    unnamed x7, local copies, waits for them, and re-layouts  2.88 us

profile of v4, /device:TPU:1, one launch (start us, length us, event | category | flops | bytes accessed | tf_op | source)
XLA Modules:
  0.0 95.0 jit_solution(10237679463867527739)
XLA Ops:
  0.6 91.5 %hss.1 = (bf16[512,128]{1,0:T(8,128)(2,1)}, f32[16,32]{1,0:T(8,128)}, f32[16,32]{1,0:T(8,128)}) custom-call(f32[3,512]{1,0:T(4,128)} %points_ref.1, s32[1,512]{1,0:T(1,128)} %bitcast.3, s32[1,512]{1,0:T(1,128)} %bitcast.4, s32[1,512]{1,0:T(1,128)} %bitcast.5, bf16[512,512]{1,0:T(8,128)(2,1)} %samp_hbm.1, s32[60,128]{1,0:T(8,128)} %skel_ref.1, s32[60]{0:T(128)} %rank_ref.1), custom_call_target="tpu_custom_call" | custom-call | tf_op jit(solution)/shard_map/hss/pallas_call | solution.py:464
  92.1 0.0 copy-start.1
  92.1 1.6 %copy.13 = bf16[512,128]{1,0:T(8,128)(2,1)} copy(bf16[512,128]{1,0:T(8,128)(2,1)} %get-tuple-element.6) | data formatting | bytes 262144
  93.7 0.0 copy-done.1
  93.7 0.0 copy-start
  93.7 0.6 copy.14
  94.3 0.1 copy-done
  94.4 0.6 copy.15
Async XLA Ops:
  92.1 1.6 %copy-start.1 = (f32[16,32]{1,0:T(8,128)S(1)}, f32[16,32]{1,0:T(8,128)}, u32[]{:S(2)}) copy-start(f32[16,32]{1,0:T(8,128)} %get-tuple-element.7) | copy-start | bytes 6148
  93.7 0.7 copy-start

commit v5 on v4

--- a/solution.py
+++ b/solution.py
@@ -12,6 +12,7 @@
 VM = pl.BlockSpec(memory_space=pltpu.VMEM)
 SM = pl.BlockSpec(memory_space=pltpu.SMEM)
 ANY = pl.BlockSpec(memory_space=pl.ANY)
+HBM = pl.BlockSpec(memory_space=pltpu.HBM)
 
 NTOTAL = 1048576
 KERNEL_SCALE = 1.0
@@ -104,10 +105,61 @@
     return gram + jnp.where(same, shift, 0.0)
 
 
+def unit8():
+    return (iota((8, LANES), 0) == iota((8, LANES), 1)).astype(BF16)
+
+
+def merge(level, leaf, pk, pp, sp, skel_ref, rank_ref):
+    leaves = lax.axis_size("leaf")
+    r = skel_ref.shape[1]
+    child_base = sum(leaves >> k for k in range(level - 1))
+    base = child_base + (leaves >> (level - 1))
+    sub = iota((r, 1), 0)
+    node = leaf // (1 << level)
+    rank_l = rank_ref[child_base + 2 * node]
+    rank_r = rank_ref[child_base + 2 * node + 1]
+    rank_p = rank_ref[base + node]
+    spots_l = exact(sp[0], unit8(), 0, 0)
+    row_r = sp[1]
+    d2 = None
+    for axis in range(3):
+        off = spots_l[:, axis : axis + 1] - row_r[axis : axis + 1, :]
+        d2 = off * off if d2 is None else d2 + off * off
+    cross = kern(d2)
+    upper = (pk[0] - mm(cross, pp[1], 1, 0, 3)) * jnp.where(sub < rank_l, 1.0, 0.0)
+    lower = (pk[1] - mm(cross, pp[0], 0, 0, 3)) * jnp.where(sub < rank_r, 1.0, 0.0)
+    cand = jnp.concatenate([upper, lower], 0)
+    spots = jnp.concatenate([sp[0], row_r], 1)
+    row = skel_ref[pl.ds(base + node, 1), :]
+    chooser = jnp.where(jnp.broadcast_to(row, (2 * r, r)) == iota((2 * r, r), 0), 1.0, 0.0).astype(BF16)
+    chosen = bdot(jnp.concatenate([chooser] * 3, 0), jnp.concatenate(split(cand, 3), 0), 0, 0)
+    return cand, spots, chooser, chosen * jnp.where(sub < rank_p, 1.0, 0.0), rank_p
+
+
+def top_kernel(basis_ref, pk, pp, sp, skel_ref, rank_ref, basis_out, top_s, top_o, pk3, ww3, sem):
+    save = pltpu.make_async_copy(basis_ref, basis_out, sem)
+    save.start()
+    leaf = lax.axis_index("leaf")
+    me = lax.axis_index("col")
+    width = pk.shape[2]
+    share, span = top_s.shape
+    cand, _, _, picked, rank = merge(LEVELS, leaf, pk, pp, sp, skel_ref, rank_ref)
+    pk3[...] = picked
+    raw = mm(cand, picked, 1, 1, 3)
+    back = mm(raw, jnp.concatenate([pp[0], pp[1]], 0), 0, 0)
+    ww3[...] = ridged(mm(picked, picked, 1, 1, 3), rank)
+    spd_inverse(ww3, lambda b: None)
+    turn = lax.rem(width - me * span, width)
+    rows = pl.ds(pl.multiple_of(lax.rem(leaf, 8) * share, share), share)
+    top_s[...] = pltpu.roll(pk3[rows, :], turn, 1)[:, 0:span]
+    top_o[...] = pltpu.roll(mm(ww3[rows, :], back, 1, 0), turn, 1)[:, 0:span]
+    save.wait()
+
+
 def hss_kernel(
     points_ref, ids_ref, signs_ref, had_ref, samp_hbm, skel_ref, rank_ref,
-    basis_ref, top_s, top_o,
-    samp, every, om_all, own_b, pick_b, res, raw_ref, part, half, mine, landed, spk, pk, sp, hh, ww, pp, pk3, hh3, ww3,
+    basis_ref, pk_out, sp_out, pp,
+    samp, every, om_all, own_b, pick_b, res, raw_ref, part, half, mine, landed, spk, pk_low, sp_low, hh, ww,
     samp_sem, g_s, g_r, gp_s, gp_r, p_s, p_r, pp_s, pp_r,
     pair_s, pair_r, rs_s, rs_r, ag_s, ag_r, ap_s, ap_r, ax_s, ax_r, axp_s, axp_r,
     xs_s, xs_r, xk_s, xk_r, xkp_s, xkp_r, xh_s, xh_r, xhp_s, xhp_r, xw_s, xw_r, xwp_s, xwp_r,
@@ -122,6 +174,10 @@
     width = had_ref.shape[1]
     r = skel_ref.shape[1]
     count = r // COLS
+    pk = [pk_low.at[0], pk_low.at[1], pk_out]
+    sp = [sp_low.at[0], sp_low.at[1], sp_out]
+    zhalf = lax.rem(z, 2)
+    zmate = (z + 1 - 2 * zhalf) * 2 + core
     sides = [lax.rem(leaf // (1 << lvl), 2) for lvl in range(LEVELS)]
     siblings = [leaf + (1 << lvl) - (2 << lvl) * sides[lvl] for lvl in range(LEVELS)]
     sends = []
@@ -162,7 +218,7 @@
     part[...] = bdot(chooser_of(me), samp[...], 0, 0)
     spk[my_rows, :] = part[my_rows, :]
 
-    ident = (iota((8, LANES), 0) == iota((8, LANES), 1)).astype(BF16)
+    ident = unit8()
     own_cols = exact(every[me], ident, 0, 0)
     for axis in range(3):
         own_b[axis] = jnp.broadcast_to(own_cols[:, axis : axis + 1], (rows, LANES))
@@ -237,8 +293,8 @@
         return spots
 
     spots = lax.fori_loop(0, ZS, near_step, jnp.zeros((8, r), F32))
-    sp[0, sides[0]] = spots
-    put(sp.at[0, sides[0]], sp.at[0, sides[0]], xs_s.at[0], xs_r.at[0], leaf=siblings[0]).start()
+    sp[0][sides[0]] = spots
+    put(sp[0].at[sides[0]], sp[0].at[sides[0]], xs_s.at[0], xs_r.at[0], leaf=siblings[0]).start()
 
     spot_cols = exact(spots, ident, 0, 0)
     for axis in range(3):
@@ -270,7 +326,7 @@
 
     lax.fori_loop(0, ZS, pick_settle, 0)
     sub = iota((r, 1), 0)
-    pk[0, sides[0]] = (spk[...] - 0.25 * part[...]) * jnp.where(sub < rank_ref[leaf], 1.0, 0.0)
+    pk[0][sides[0]] = (spk[...] - 0.25 * part[...]) * jnp.where(sub < rank_ref[leaf], 1.0, 0.0)
 
     def pieces(buf, level, side, chunks, half_of):
         size = r // 2 // chunks
@@ -289,18 +345,48 @@
         for q, piece in enumerate(pieces(buf, level, 1 - sides[level], chunks, 1 - core)):
             put(piece, piece, s2.at[level, q], rv2.at[level, q], keep=False, col=partner).wait_recv()
 
+    def quarter(level, side, half_of, chip):
+        size = r // 4
+        return pk[level].at[side, pl.ds(pl.multiple_of((half_of * 2 + chip) * size, size), size)]
+
+    def offer_picked(level):
+        piece = quarter(level, sides[level], core, zhalf)
+        put(piece, piece, xk_s.at[level, 0], xk_r.at[level, 0], leaf=siblings[level]).start()
+
+    def relay_picked(level):
+        got = quarter(level, 1 - sides[level], core, zhalf)
+        put(got, got, xk_s.at[level, 0], xk_r.at[level, 0], keep=False, leaf=siblings[level]).wait_recv()
+        put(got, got, xk_s.at[level, 1], xk_r.at[level, 1], keep=False, col=zmate).start()
+        put(got, got, xkp_s.at[level, 0], xkp_r.at[level, 0], keep=False, col=partner).start()
+
+    def relay_picked_mate(level):
+        got = quarter(level, 1 - sides[level], core, 1 - zhalf)
+        put(got, got, xk_s.at[level, 1], xk_r.at[level, 1], keep=False, col=zmate).wait_recv()
+        put(got, got, xkp_s.at[level, 1], xkp_r.at[level, 1], keep=False, col=partner).start()
+
+    def settle_picked(level):
+        for q, chip in enumerate((zhalf, 1 - zhalf)):
+            got = quarter(level, 1 - sides[level], 1 - core, chip)
+            put(got, got, xkp_s.at[level, q], xkp_r.at[level, q], keep=False, col=partner).wait_recv()
+
+    def drain_picked(level):
+        got = quarter(level, 1 - sides[level], core, zhalf)
+        put(got, got, xk_s.at[level, 1], xk_r.at[level, 1], keep=False, col=zmate).wait_send()
+        for q in range(2):
+            put(got, got, xkp_s.at[level, q], xkp_r.at[level, q], keep=False, col=partner).wait_send()
+
     def hear(level):
-        got = sp.at[level, 1 - sides[level]]
+        got = sp[level].at[1 - sides[level]]
         put(got, got, xs_s.at[level], xs_r.at[level], keep=False, leaf=siblings[level]).wait_recv()
 
     def drain_relay(buf, level, chunks, s2, rv2):
         for q, piece in enumerate(pieces(buf, level, 1 - sides[level], chunks, core)):
             put(piece, piece, s2.at[level, q], rv2.at[level, q], keep=False, col=partner).wait_send()
 
-    offer(pk, 0, 2, xk_s, xk_r)
+    offer_picked(0)
 
     side0 = sides[0]
-    picked = pk[0, side0]
+    picked = pk[0][side0]
     raw = mm(res[...], picked, 1, 1)
     raw_ref[...] = raw
     om_own = om_all[me]
@@ -326,7 +412,7 @@
 
         @pl.when(b == 6)
         def _():
-            relay(pk, 0, 2, xk_s, xk_r, xkp_s, xkp_r)
+            relay_picked(0)
 
     spd_inverse(ww.at[0, side0], leaf_hook)
     offer(ww, 0, 1, xw_s, xw_r)
@@ -350,6 +436,7 @@
         put(got, got, ag_s.at[off], ag_r.at[off], keep=False, col=partner).wait_recv()
         put(got, got, ap_s.at[off], ap_r.at[off], col=partner).start()
         put(got, got, ax_s.at[off], ax_r.at[off], leaf=siblings[0]).start()
+    relay_picked_mate(0)
     relay(ww, 0, 1, xw_s, xw_r, xwp_s, xwp_r)
     for off in (0, 1, 7, 2, 6, 3, 5, 4):
         got = n_rows(1 - side0, core, zpeer(off))
@@ -359,7 +446,7 @@
         got = n_rows(side0, 1 - core, zpeer(off))
         put(got, got, ap_s.at[off], ap_r.at[off], keep=False, col=partner).wait_recv()
     pp[side0] = mm(ww[0, side0], hh[0, side0], 1, 0)
-    settle(pk, 0, 2, xkp_s, xkp_r)
+    settle_picked(0)
     hear(0)
     settle(ww, 0, 1, xwp_s, xwp_r)
     for off in range(ZS):
@@ -367,82 +454,42 @@
         put(got, got, axp_s.at[off], axp_r.at[off], keep=False, col=partner).wait_recv()
     pp[1 - side0] = mm(ww[0, 1 - side0], hh[0, 1 - side0], 1, 0)
 
-    child_base = 0
-    base = 0
-    for level in range(1, LEVELS + 1):
-        child_base, base = base, base + leaves // (1 << (level - 1))
-        node = leaf // (1 << level)
-        rank_l = rank_ref[child_base + 2 * node]
-        rank_r = rank_ref[child_base + 2 * node + 1]
-        rank_p = rank_ref[base + node]
-        spots_l = exact(sp[level - 1, 0], ident, 0, 0)
-        row_r = sp[level - 1, 1]
-        d2 = None
-        for axis in range(3):
-            off = spots_l[:, axis : axis + 1] - row_r[axis : axis + 1, :]
-            d2 = off * off if d2 is None else d2 + off * off
-        cross = kern(d2)
-        proj_l, proj_r = pp[0], pp[1]
-        upper = (pk[level - 1, 0] - mm(cross, proj_r, 1, 0, 3)) * jnp.where(sub < rank_l, 1.0, 0.0)
-        lower = (pk[level - 1, 1] - mm(cross, proj_l, 0, 0, 3)) * jnp.where(sub < rank_r, 1.0, 0.0)
-        cand = jnp.concatenate([upper, lower], 0)
-        spots = jnp.concatenate([sp[level - 1, 0], row_r], 1)
-        row = skel_ref[pl.ds(base + node, 1), :]
-        chooser = jnp.where(jnp.broadcast_to(row, (2 * r, r)) == iota((2 * r, r), 0), 1.0, 0.0).astype(BF16)
-        three = split(cand, 3)
-        chosen = bdot(jnp.concatenate([chooser] * 3, 0), jnp.concatenate(three, 0), 0, 0)
-        picked = chosen * jnp.where(sub < rank_p, 1.0, 0.0)
-        last = level == LEVELS
-        if not last:
-            side = sides[level]
-            pk[level, side] = picked
-            sp[level, side] = exact(spots, chooser, 1, 0)
-            offer(pk, level, 2, xk_s, xk_r)
-            put(sp.at[level, side], sp.at[level, side], xs_s.at[level], xs_r.at[level], leaf=siblings[level]).start()
-        else:
-            pk3[...] = picked
+    for level in range(1, LEVELS):
+        side = sides[level]
+        cand, spots, chooser, picked, rank = merge(level, leaf, pk[level - 1], pp, sp[level - 1], skel_ref, rank_ref)
+        pk[level][side] = picked
+        offer_picked(level)
+        sp[level][side] = exact(spots, chooser, 1, 0)
+        put(sp[level].at[side], sp[level].at[side], xs_s.at[level], xs_r.at[level], leaf=siblings[level]).start()
         raw = mm(cand, picked, 1, 1, 3)
-        back = mm(raw, jnp.concatenate([proj_l, proj_r], 0), 0, 0)
-        if not last:
-            hh[level, side] = back
-            offer(hh, level, 2, xh_s, xh_r)
-        else:
-            hh3[...] = back
-        gram = ridged(mm(picked, picked, 1, 1, 3), rank_p)
-        if not last:
-            ww[level, side] = gram
-
-            def hook(b, level=level):
-                @pl.when(b == 4)
-                def _():
-                    relay(pk, level, 2, xk_s, xk_r, xkp_s, xkp_r)
-
-            spd_inverse(ww.at[level, side], hook)
-            offer(ww, level, 1, xw_s, xw_r)
-            pp[side] = mm(ww[level, side], hh[level, side], 1, 0)
-            relay(hh, level, 2, xh_s, xh_r, xhp_s, xhp_r)
-            relay(ww, level, 1, xw_s, xw_r, xwp_s, xwp_r)
-            settle(pk, level, 2, xkp_s, xkp_r)
-            hear(level)
-            settle(hh, level, 2, xhp_s, xhp_r)
-            settle(ww, level, 1, xwp_s, xwp_r)
-            pp[1 - side] = mm(ww[level, 1 - side], hh[level, 1 - side], 1, 0)
-        else:
-            ww3[...] = gram
-            spd_inverse(ww3, lambda b: None)
-            share, span = top_s.shape
-            turn = lax.rem(width - me * span, width)
-            mine_rows = pl.ds(pl.multiple_of(lax.rem(leaf, 8) * share, share), share)
-            top_s[...] = pltpu.roll(pk3[mine_rows, :], turn, 1)[:, 0:span]
-            top_o[...] = pltpu.roll(mm(ww3[mine_rows, :], hh3[...], 1, 0), turn, 1)[:, 0:span]
+        hh[level, side] = mm(raw, jnp.concatenate([pp[0], pp[1]], 0), 0, 0)
+        offer(hh, level, 4, xh_s, xh_r)
+        ww[level, side] = ridged(mm(picked, picked, 1, 1, 3), rank)
+
+        def hook(b, level=level):
+            @pl.when(b == 5)
+            def _():
+                relay_picked(level)
+
+        spd_inverse(ww.at[level, side], hook)
+        offer(ww, level, 1, xw_s, xw_r)
+        pp[side] = mm(ww[level, side], hh[level, side], 1, 0)
+        relay_picked_mate(level)
+        relay(hh, level, 4, xh_s, xh_r, xhp_s, xhp_r)
+        relay(ww, level, 1, xw_s, xw_r, xwp_s, xwp_r)
+        settle_picked(level)
+        hear(level)
+        settle(hh, level, 4, xhp_s, xhp_r)
+        settle(ww, level, 1, xwp_s, xwp_r)
+        pp[1 - side] = mm(ww[level, 1 - side], hh[level, 1 - side], 1, 0)
 
     for copy in sends:
         copy.wait_send()
     for level in range(LEVELS):
-        drain_relay(pk, level, 2, xkp_s, xkp_r)
+        drain_picked(level)
         drain_relay(ww, level, 1, xwp_s, xwp_r)
         if level > 0:
-            drain_relay(hh, level, 2, xhp_s, xhp_r)
+            drain_relay(hh, level, 4, xhp_s, xhp_r)
 
     def drain(t, carry):
         same = zpeer(zorder(t)) * 2 + core
@@ -460,16 +507,21 @@
     count = r // COLS
     shape = jax.ShapeDtypeStruct
     fetched = pltpu.VMEM
-    sems = [DMA(()), *[DMA((ZS,))] * 8, DMA(()), DMA(()), *[DMA((ZS,))] * 10, *[DMA((LEVELS,))] * 2, *[DMA((LEVELS, 2))] * 12]
-    return pl.pallas_call(
+    pair_of = [DMA((LEVELS, 2))] * 4
+    sems = [
+        DMA(()), *[DMA((ZS,))] * 8, DMA(()), DMA(()), *[DMA((ZS,))] * 10, *[DMA((LEVELS,))] * 2,
+        *pair_of, *[DMA((LEVELS, 4))] * 4, *pair_of,
+    ]
+    basis, pk, sp, pp = pl.pallas_call(
         hss_kernel,
         out_shape=[
             shape((rows, r), BF16),
-            shape((r // 8, width // COLS), F32),
-            shape((r // 8, width // COLS), F32),
+            shape((2, r, width), F32),
+            shape((2, 8, r), F32),
+            shape((2, r, width), F32),
         ],
-        in_specs=[VM, VM, VM, VM, ANY, VM, SM],
-        out_specs=[VM] * 3,
+        in_specs=[VM, VM, VM, VM, HBM, VM, SM],
+        out_specs=[VM] * 4,
         scratch_shapes=[
             fetched((rows, width), BF16),
             fetched((COLS, 8, rows), F32),
@@ -483,19 +535,27 @@
             fetched((r // 2, width), F32),
             fetched((ZS - 1, count, width), F32),
             fetched((r, width), F32),
-            fetched((LEVELS, 2, r, width), F32),
-            fetched((LEVELS, 2, 8, r), F32),
+            fetched((2, 2, r, width), F32),
+            fetched((2, 2, 8, r), F32),
             fetched((LEVELS, 2, r, width), F32),
             fetched((LEVELS, 2, r, r), F32),
-            fetched((2, r, width), F32),
-            fetched((r, width), F32),
-            fetched((r, width), F32),
-            fetched((r, r), F32),
             *sems,
         ],
-        compiler_params=pltpu.CompilerParams(collective_id=0, has_side_effects=True),
+        compiler_params=pltpu.CompilerParams(
+            collective_id=0, has_side_effects=True, vmem_limit_bytes=32 * 1024 * 1024
+        ),
         name="hss",
     )(points, point_ids[None], signs[None], hadamard_sample_rows[None], samples, skeleton, ranks)
+    top = shape((r // 8, width // COLS), F32)
+    return pl.pallas_call(
+        top_kernel,
+        out_shape=[shape((rows, r), BF16), top, top],
+        in_specs=[VM, VM, VM, VM, VM, SM],
+        out_specs=[ANY, VM, VM],
+        scratch_shapes=[fetched((r, width), F32), fetched((r, r), F32), DMA(())],
+        compiler_params=pltpu.CompilerParams(vmem_limit_bytes=32 * 1024 * 1024),
+        name="top",
+    )(basis, pk, pp, sp, skeleton, ranks)
 
 
 def solution(mesh):

time: 95.3 us -> 95 us (level)
  Pallas kernels: 91.5 us -> 90.1 us
  local copies, waits for them, and re-layouts: 2.88 us -> 3.85 us
    pallas_call x1 -> x2, Pallas kernels: 91.5 us -> 90.1 us  [the longest x1 81.8 us: local(): pl.pallas_call(hss_kernel, out_shape=[shape((rows, r), BF16), shape((2, r...]
    unnamed x7 -> x14, local copies, waits for them, and re-layouts: 2.88 us -> 3.85 us
where the time goes in v5:
time: 95 us; the launch traced here: 94.7 us
  Pallas kernels  90.1 us (95%)
  local copies, waits for them, and re-layouts  3.85 us (4%)
    pallas_call x1, Pallas kernels, local(): pl.pallas_call(hss_kernel, out_shape=[shape((rows, r), BF16), shape((2, r...  81.8 us
    pallas_call x1, Pallas kernels, local(): pl.pallas_call(top_kernel, out_shape=[shape((rows, r), BF16), top, top],...  8.29 us
    unnamed x14, local copies, waits for them, and re-layouts  3.85 us

profile of v5, /device:TPU:1, one launch (start us, length us, event | category | flops | bytes accessed | tf_op | source)
XLA Modules:
  0.0 94.7 jit_solution(18371807033382261720)
XLA Ops:
  0.6 0.0 copy-start.4
  0.6 0.0 copy-start.3
  0.7 0.0 copy-start.6
  0.7 0.7 copy-done.4
  1.3 0.0 copy-done.3
  1.3 0.0 copy-done.6
  1.3 0.0 copy-start
  1.3 1.0 %copy-done = bf16[512,512]{1,0:T(8,128)(2,1)S(1)} copy-done((bf16[512,512]{1,0:T(8,128)(2,1)S(1)}, bf16[512,512]{1,0:T(8,128)(2,1)}, u32[]{:S(2)}) %copy-start) | copy-done | bytes 524312
  2.4 0.0 copy-start.1
  2.4 0.8 copy-done.1
  3.1 0.0 copy-start.2
  3.1 0.7 copy-done.2
  3.8 0.0 copy-start.5
  3.8 0.7 copy-done.5
  4.5 81.8 %hss.1 = (bf16[512,128]{1,0:T(8,128)(2,1)S(1)}, f32[2,128,512]{2,1,0:T(8,128)S(1)}, f32[2,8,128]{2,1,0:T(8,128)S(1)}, f32[2,128,512]{2,1,0:T(8,128)S(1)}) custom-call(f32[3,512]{1,0:T(4,128)S(1)} %copy-done.2, s32[1,512]{1,0:T(1,128)S(1)} %bitcast.3, s32[1,512]{1,0:T(1,128)S(1)} %bitcast.4, s32[1,512]{1,0:T(1,128)S(1)} %bitcast.5, ...), custom_call_target="tpu_custom_call" | custom-call | tf_op jit(solution)/shard_map/hss/pallas_call | solution.py:515
  86.4 8.3 %top.1 = (bf16[512,128]{1,0:T(8,128)(2,1)}, f32[16,32]{1,0:T(8,128)}, f32[16,32]{1,0:T(8,128)}) custom-call(bf16[512,128]{1,0:T(8,128)(2,1)S(1)} %get-tuple-element.7.basis_ref, f32[2,128,512]{2,1,0:T(8,128)S(1)} %get-tuple-element.8.pk, f32[2,128,512]{2,1,0:T(8,128)S(1)} %get-tuple-element.9.pp, f32[2,8,128]{2,1,0:T(8,128)S(1)} %get-tuple-element.10.sp, ...), custom_call_target="tpu_custom_call" | custom-call | tf_op jit(solution)/shard_map/top/pallas_call | solution.py:550
Async XLA Ops:
  0.6 0.7 copy-start.4
  0.6 0.7 copy-start.3
  0.7 0.7 copy-start.6
  1.3 1.0 %copy-start = (bf16[512,512]{1,0:T(8,128)(2,1)S(1)}, bf16[512,512]{1,0:T(8,128)(2,1)}, u32[]{:S(2)}) copy-start(bf16[512,512]{1,0:T(8,128)(2,1)} %samp_hbm.1) | copy-start | bytes 1572868
  2.4 0.8 copy-start.1
  3.1 0.7 copy-start.2
  3.8 0.7 copy-start.5

commit v6 on v5

--- a/solution.py
+++ b/solution.py
@@ -157,9 +157,9 @@
 
 
 def hss_kernel(
-    points_ref, ids_ref, signs_ref, had_ref, samp_hbm, skel_ref, rank_ref,
+    points_hbm, ids_hbm, signs_hbm, had_hbm, samp_hbm, skel_hbm, rank_hbm,
     basis_ref, pk_out, sp_out, pp,
-    samp, every, om_all, own_b, pick_b, res, raw_ref, part, half, mine, landed, spk, pk_low, sp_low, hh, ww,
+    points_ref, ids_ref, signs_ref, had_ref, skel_ref, rank_ref, samp, every, om_all, own_b, pick_b, res, raw_ref, part, half, mine, landed, spk, pk_low, sp_low, hh, ww,
     samp_sem, g_s, g_r, gp_s, gp_r, p_s, p_r, pp_s, pp_r,
     pair_s, pair_r, rs_s, rs_r, ag_s, ag_r, ap_s, ap_r, ax_s, ax_r, axp_s, axp_r,
     xs_s, xs_r, xk_s, xk_r, xkp_s, xkp_r, xh_s, xh_r, xhp_s, xhp_r, xw_s, xw_r, xwp_s, xwp_r,
@@ -193,14 +193,30 @@
     def zpeer(off):
         return lax.rem(z + off, ZS)
 
-    fetch = pltpu.make_async_copy(samp_hbm, samp, samp_sem)
-    fetch.start()
+    fetches = [
+        pltpu.make_async_copy(source, target, samp_sem.at[i])
+        for i, (source, target) in enumerate(
+            (
+                (points_hbm, points_ref),
+                (ids_hbm, ids_ref),
+                (signs_hbm, signs_ref),
+                (skel_hbm, skel_ref),
+                (rank_hbm, rank_ref),
+                (had_hbm, had_ref),
+                (samp_hbm, samp),
+            )
+        )
+    ]
+    for fetch in fetches:
+        fetch.start()
     barrier = pltpu.get_barrier_semaphore()
     for off in range(1, ZS):
         pl.semaphore_signal(barrier, inc=1, device_id={"col": zpeer(off) * 2 + core}, device_id_type=MESH)
     pl.semaphore_signal(barrier, inc=1, device_id={"col": partner}, device_id_type=MESH)
     for sibling in siblings:
         pl.semaphore_signal(barrier, inc=1, device_id={"leaf": sibling}, device_id_type=MESH)
+    for fetch in fetches:
+        fetch.wait()
     every[me, 0:3, :] = points_ref[...]
     every[me, 3:4, :] = ids_ref[...].astype(F32)
     every[me, 4:5, :] = signs_ref[...].astype(F32)
@@ -214,7 +230,6 @@
             jnp.broadcast_to(entry - slot * rows, (rows, r)) == iota((rows, r), 0), 1.0, 0.0
         ).astype(BF16)
 
-    fetch.wait()
     part[...] = bdot(chooser_of(me), samp[...], 0, 0)
     spk[my_rows, :] = part[my_rows, :]
 
@@ -507,9 +522,10 @@
     count = r // COLS
     shape = jax.ShapeDtypeStruct
     fetched = pltpu.VMEM
+    inputs = [points, point_ids[None], signs[None], hadamard_sample_rows[None], samples, skeleton, ranks]
     pair_of = [DMA((LEVELS, 2))] * 4
     sems = [
-        DMA(()), *[DMA((ZS,))] * 8, DMA(()), DMA(()), *[DMA((ZS,))] * 10, *[DMA((LEVELS,))] * 2,
+        DMA((7,)), *[DMA((ZS,))] * 8, DMA(()), DMA(()), *[DMA((ZS,))] * 10, *[DMA((LEVELS,))] * 2,
         *pair_of, *[DMA((LEVELS, 4))] * 4, *pair_of,
     ]
     basis, pk, sp, pp = pl.pallas_call(
@@ -520,9 +536,15 @@
             shape((2, 8, r), F32),
             shape((2, r, width), F32),
         ],
-        in_specs=[VM, VM, VM, VM, HBM, VM, SM],
+        in_specs=[HBM] * 7,
         out_specs=[VM] * 4,
         scratch_shapes=[
+            fetched((3, rows), F32),
+            fetched((1, rows), jnp.int32),
+            fetched((1, rows), jnp.int32),
+            fetched((1, width), jnp.int32),
+            fetched(skeleton.shape, jnp.int32),
+            pltpu.SMEM(ranks.shape, jnp.int32),
             fetched((rows, width), BF16),
             fetched((COLS, 8, rows), F32),
             fetched((COLS, rows, width), BF16),
@@ -545,7 +567,7 @@
             collective_id=0, has_side_effects=True, vmem_limit_bytes=32 * 1024 * 1024
         ),
         name="hss",
-    )(points, point_ids[None], signs[None], hadamard_sample_rows[None], samples, skeleton, ranks)
+    )(*[pltpu.with_memory_space_constraint(x, pltpu.HBM) for x in inputs])
     top = shape((r // 8, width // COLS), F32)
     return pl.pallas_call(
         top_kernel,

time: 95 us -> 91.4 us (0.962)
  local copies, waits for them, and re-layouts: 3.85 us -> 0.64 us
    unnamed x14 -> x4, local copies, waits for them, and re-layouts: 3.85 us -> 0.64 us
where the time goes in v6:
time: 91.4 us; the launch traced here: 91.2 us
  Pallas kernels  89.9 us (98%)
    pallas_call x1, Pallas kernels, local(): pl.pallas_call(hss_kernel, out_shape=[shape((rows, r), BF16), shape((2, r...  81.6 us
    pallas_call x1, Pallas kernels, local(): pl.pallas_call(top_kernel, out_shape=[shape((rows, r), BF16), top, top],...  8.29 us

profile of v6, /device:TPU:1, one launch (start us, length us, event | category | flops | bytes accessed | tf_op | source)
XLA Modules:
  0.0 91.2 jit_solution(5375425841192022979)
XLA Ops:
  0.6 0.0 copy-start
  0.6 81.6 %hss.1 = (bf16[512,128]{1,0:T(8,128)(2,1)S(1)}, f32[2,128,512]{2,1,0:T(8,128)S(1)}, f32[2,8,128]{2,1,0:T(8,128)S(1)}, f32[2,128,512]{2,1,0:T(8,128)S(1)}) custom-call(f32[3,512]{1,0:T(4,128)} %points_hbm.1, s32[1,512]{1,0:T(1,128)} %bitcast.3, s32[1,512]{1,0:T(1,128)} %bitcast.4, s32[1,512]{1,0:T(1,128)} %bitcast.5, bf16[512,512]{1,0:T(8,128)(2,1)} %samp_hbm.1, ...), custom_call_target="tpu_custom_call" | custom-call | tf_op jit(solution)/shard_map/hss/pallas_call | solution.py:531
  82.3 0.0 copy-start.1
  82.3 0.0 copy-done
  82.3 0.6 copy-done.1
  82.9 8.3 %top.1 = (bf16[512,128]{1,0:T(8,128)(2,1)}, f32[16,32]{1,0:T(8,128)}, f32[16,32]{1,0:T(8,128)}) custom-call(bf16[512,128]{1,0:T(8,128)(2,1)S(1)} %get-tuple-element.7.basis_ref, f32[2,128,512]{2,1,0:T(8,128)S(1)} %get-tuple-element.8.pk, f32[2,128,512]{2,1,0:T(8,128)S(1)} %get-tuple-element.9.pp, f32[2,8,128]{2,1,0:T(8,128)S(1)} %get-tuple-element.10.sp, ...), custom_call_target="tpu_custom_call" | custom-call | tf_op jit(solution)/shard_map/top/pallas_call | solution.py:572
Async XLA Ops:
  0.6 81.7 %copy-start = (s32[60,128]{1,0:T(8,128)S(1)}, s32[60,128]{1,0:T(8,128)}, u32[]{:S(2)}) copy-start(s32[60,128]{1,0:T(8,128)} %skel_ref.1) | copy-start | bytes 92164
  82.3 0.7 copy-start.1

commit v7 on v6

--- a/solution.py
+++ b/solution.py
@@ -62,7 +62,7 @@
     return jnp.exp2(squared_distance * (-KERNEL_SCALE * LOG2E))
 
 
-def spd_inverse(a_ref, hook):
+def spd_inverse(a_ref, scale, hook):
     n = a_ref.shape[0]
     lane = iota((PANEL, n), 1)
     sub = iota((PANEL, n), 0)
@@ -75,15 +75,22 @@
         rolled = pltpu.roll(panel, lax.rem(n - start, n), 1)
         diag = [jnp.broadcast_to(rolled[:, k : k + 1], (PANEL, n)) for k in range(PANEL)]
         rows = jnp.where(lane < PANEL, ident, rolled)
-        for k in range(PANEL):
-            inv = 1.0 / diag[k][k : k + 1, :]
-            here = sub == k
-            factor = diag[k] * inv
-            for j in range(k + 1, PANEL):
-                own = diag[j][k : k + 1, :]
-                diag[j] = jnp.where(here, own * inv, diag[j] - factor * own)
-            own = rows[k : k + 1, :]
-            rows = jnp.where(here, own * inv, rows - factor * own)
+        for k in range(0, PANEL, 2):
+            one, two = diag[k], diag[k + 1]
+            a, c = one[k : k + 1, :], two[k + 1 : k + 2, :]
+            low, up = one[k + 1 : k + 2, :], two[k : k + 1, :]
+            inv = 1.0 / (a * c - low * up)
+            first, second = sub == k, sub == k + 1
+            g0 = jnp.where(first, -c, jnp.where(second, low, one * c - two * low))
+            g1 = jnp.where(first, up, jnp.where(second, -a, two * a - one * up))
+
+            def sweep(x):
+                base = jnp.where(first | second, 0.0, x)
+                return base - (g0 * x[k : k + 1, :] + g1 * x[k + 1 : k + 2, :]) * inv
+
+            for j in range(k + 2, PANEL):
+                diag[j] = sweep(diag[j])
+            rows = sweep(rows)
         rows = pltpu.roll(rows, start, 1)
         side = jnp.where(lane < start, -panel, panel)
         side = jnp.where((lane >= start) & (lane < start + PANEL), 0.0, side)
@@ -95,6 +102,7 @@
         return carry
 
     lax.fori_loop(0, n // PANEL, step, 0)
+    a_ref[...] = a_ref[...] * scale
 
 
 def ridged(gram, rank):
@@ -102,7 +110,8 @@
     same = iota((n, n), 0) == iota((n, n), 1)
     trace = jnp.sum(jnp.where(same, gram, 0.0), keepdims=True)
     shift = RIDGE * trace / rank.astype(F32) + 1e-06
-    return gram + jnp.where(same, shift, 0.0)
+    scale = 1.0 / shift
+    return gram * scale + jnp.where(same, 1.0, 0.0), scale
 
 
 def unit8():
@@ -136,9 +145,17 @@
     return cand, spots, chooser, chosen * jnp.where(sub < rank_p, 1.0, 0.0), rank_p
 
 
-def top_kernel(basis_ref, pk, pp, sp, skel_ref, rank_ref, basis_out, top_s, top_o, pk3, ww3, sem):
-    save = pltpu.make_async_copy(basis_ref, basis_out, sem)
+def top_kernel(basis_ref, pk, pp, sp, skel_hbm, rank_hbm, basis_out, top_s, top_o, skel_ref, rank_ref, pk3, ww3, sem):
+    fetches = [
+        pltpu.make_async_copy(rank_hbm, rank_ref, sem.at[1]),
+        pltpu.make_async_copy(skel_hbm, skel_ref, sem.at[2]),
+    ]
+    for fetch in fetches:
+        fetch.start()
+    save = pltpu.make_async_copy(basis_ref, basis_out, sem.at[0])
     save.start()
+    for fetch in fetches:
+        fetch.wait()
     leaf = lax.axis_index("leaf")
     me = lax.axis_index("col")
     width = pk.shape[2]
@@ -147,8 +164,8 @@
     pk3[...] = picked
     raw = mm(cand, picked, 1, 1, 3)
     back = mm(raw, jnp.concatenate([pp[0], pp[1]], 0), 0, 0)
-    ww3[...] = ridged(mm(picked, picked, 1, 1, 3), rank)
-    spd_inverse(ww3, lambda b: None)
+    ww3[...], scale = ridged(mm(picked, picked, 1, 1, 3), rank)
+    spd_inverse(ww3, scale, lambda b: None)
     turn = lax.rem(width - me * span, width)
     rows = pl.ds(pl.multiple_of(lax.rem(leaf, 8) * share, share), share)
     top_s[...] = pltpu.roll(pk3[rows, :], turn, 1)[:, 0:span]
@@ -411,7 +428,7 @@
     other0 = pl.multiple_of((1 - core) * r2, r2)
     pair = put(part.at[pl.ds(other0, r2)], half, pair_s, pair_r, col=partner)
     pair.start()
-    ww[0, side0] = ridged(mm(picked, picked, 1, 1), rank_ref[leaf])
+    ww[0, side0], scale = ridged(mm(picked, picked, 1, 1), rank_ref[leaf])
     scatter = []
     for off in range(1, ZS):
         piece = pl.ds(pl.multiple_of(zpeer(off) * count, count), count)
@@ -429,7 +446,7 @@
         def _():
             relay_picked(0)
 
-    spd_inverse(ww.at[0, side0], leaf_hook)
+    spd_inverse(ww.at[0, side0], scale, leaf_hook)
     offer(ww, 0, 1, xw_s, xw_r)
     basis_ref[...] = mm(raw_ref[...], ww[0, side0], 1, 0).astype(BF16)
 
@@ -479,14 +496,14 @@
         raw = mm(cand, picked, 1, 1, 3)
         hh[level, side] = mm(raw, jnp.concatenate([pp[0], pp[1]], 0), 0, 0)
         offer(hh, level, 4, xh_s, xh_r)
-        ww[level, side] = ridged(mm(picked, picked, 1, 1, 3), rank)
+        ww[level, side], scale = ridged(mm(picked, picked, 1, 1, 3), rank)
 
         def hook(b, level=level):
             @pl.when(b == 5)
             def _():
                 relay_picked(level)
 
-        spd_inverse(ww.at[level, side], hook)
+        spd_inverse(ww.at[level, side], scale, hook)
         offer(ww, level, 1, xw_s, xw_r)
         pp[side] = mm(ww[level, side], hh[level, side], 1, 0)
         relay_picked_mate(level)
@@ -572,12 +589,18 @@
     return pl.pallas_call(
         top_kernel,
         out_shape=[shape((rows, r), BF16), top, top],
-        in_specs=[VM, VM, VM, VM, VM, SM],
+        in_specs=[VM, VM, VM, VM, HBM, HBM],
         out_specs=[ANY, VM, VM],
-        scratch_shapes=[fetched((r, width), F32), fetched((r, r), F32), DMA(())],
+        scratch_shapes=[
+            fetched(skeleton.shape, jnp.int32),
+            pltpu.SMEM(ranks.shape, jnp.int32),
+            fetched((r, width), F32),
+            fetched((r, r), F32),
+            DMA((3,)),
+        ],
         compiler_params=pltpu.CompilerParams(vmem_limit_bytes=32 * 1024 * 1024),
         name="top",
-    )(basis, pk, pp, sp, skeleton, ranks)
+    )(basis, pk, pp, sp, *[pltpu.with_memory_space_constraint(x, pltpu.HBM) for x in (skeleton, ranks)])
 
 
 def solution(mesh):

time: 91.4 us -> 90.4 us (0.989)
  no operation moved by 1% of the time
where the time goes in v7:
time: 90.4 us; the launch traced here: 90.2 us
  Pallas kernels  89.6 us (99%)
    pallas_call x1, Pallas kernels, local(): pl.pallas_call(hss_kernel, out_shape=[shape((rows, r), BF16), shape((2, r...  81.2 us
    pallas_call x1, Pallas kernels, local(): pl.pallas_call(top_kernel, out_shape=[shape((rows, r), BF16), top, top],...  8.35 us

profile of v7, /device:TPU:1, one launch (start us, length us, event | category | flops | bytes accessed | tf_op | source)
XLA Modules:
  0.0 90.2 jit_solution(2393507367202168742)
XLA Ops:
  0.6 81.2 %hss.1 = (bf16[512,128]{1,0:T(8,128)(2,1)S(1)}, f32[2,128,512]{2,1,0:T(8,128)S(1)}, f32[2,8,128]{2,1,0:T(8,128)S(1)}, f32[2,128,512]{2,1,0:T(8,128)S(1)}) custom-call(f32[3,512]{1,0:T(4,128)} %points_hbm.1, s32[1,512]{1,0:T(1,128)} %bitcast.3, s32[1,512]{1,0:T(1,128)} %bitcast.4, s32[1,512]{1,0:T(1,128)} %bitcast.5, bf16[512,512]{1,0:T(8,128)(2,1)} %samp_hbm.1, ...), custom_call_target="tpu_custom_call" | custom-call | tf_op jit(solution)/shard_map/hss/pallas_call | solution.py:548
  81.8 8.4 %top.1 = (bf16[512,128]{1,0:T(8,128)(2,1)}, f32[16,32]{1,0:T(8,128)}, f32[16,32]{1,0:T(8,128)}) custom-call(bf16[512,128]{1,0:T(8,128)(2,1)S(1)} %get-tuple-element.7.basis_ref, f32[2,128,512]{2,1,0:T(8,128)S(1)} %get-tuple-element.8.pk, f32[2,128,512]{2,1,0:T(8,128)S(1)} %get-tuple-element.9.pp, f32[2,8,128]{2,1,0:T(8,128)S(1)} %get-tuple-element.10.sp, ...), custom_call_target="tpu_custom_call" | custom-call | tf_op jit(solution)/shard_map/top/pallas_call | solution.py:589

commit v8 on v7

--- a/solution.py
+++ b/solution.py
@@ -118,16 +118,19 @@
     return (iota((8, LANES), 0) == iota((8, LANES), 1)).astype(BF16)
 
 
-def merge(level, leaf, pk, pp, sp, skel_ref, rank_ref):
+def node_of(level, leaf, skel_ref, rank_ref):
     leaves = lax.axis_size("leaf")
-    r = skel_ref.shape[1]
     child_base = sum(leaves >> k for k in range(level - 1))
     base = child_base + (leaves >> (level - 1))
+    node = leaf // (1 << level)
+    ranks = (rank_ref[child_base + 2 * node], rank_ref[child_base + 2 * node + 1], rank_ref[base + node])
+    return skel_ref[pl.ds(base + node, 1), :], ranks
+
+
+def merge(row, ranks, pk, pp, sp):
+    rank_l, rank_r, rank_p = ranks
+    r = row.shape[1]
     sub = iota((r, 1), 0)
-    node = leaf // (1 << level)
-    rank_l = rank_ref[child_base + 2 * node]
-    rank_r = rank_ref[child_base + 2 * node + 1]
-    rank_p = rank_ref[base + node]
     spots_l = exact(sp[0], unit8(), 0, 0)
     row_r = sp[1]
     d2 = None
@@ -139,32 +142,24 @@
     lower = (pk[1] - mm(cross, pp[0], 0, 0, 3)) * jnp.where(sub < rank_r, 1.0, 0.0)
     cand = jnp.concatenate([upper, lower], 0)
     spots = jnp.concatenate([sp[0], row_r], 1)
-    row = skel_ref[pl.ds(base + node, 1), :]
     chooser = jnp.where(jnp.broadcast_to(row, (2 * r, r)) == iota((2 * r, r), 0), 1.0, 0.0).astype(BF16)
     chosen = bdot(jnp.concatenate([chooser] * 3, 0), jnp.concatenate(split(cand, 3), 0), 0, 0)
-    return cand, spots, chooser, chosen * jnp.where(sub < rank_p, 1.0, 0.0), rank_p
-
-
-def top_kernel(basis_ref, pk, pp, sp, skel_hbm, rank_hbm, basis_out, top_s, top_o, skel_ref, rank_ref, pk3, ww3, sem):
-    fetches = [
-        pltpu.make_async_copy(rank_hbm, rank_ref, sem.at[1]),
-        pltpu.make_async_copy(skel_hbm, skel_ref, sem.at[2]),
-    ]
-    for fetch in fetches:
-        fetch.start()
-    save = pltpu.make_async_copy(basis_ref, basis_out, sem.at[0])
+    return cand, spots, chooser, chosen * jnp.where(sub < rank_p, 1.0, 0.0)
+
+
+def top_kernel(basis_ref, pk, pp, sp, meta, basis_out, top_s, top_o, pk3, ww3, sem):
+    save = pltpu.make_async_copy(basis_ref, basis_out, sem)
     save.start()
-    for fetch in fetches:
-        fetch.wait()
     leaf = lax.axis_index("leaf")
     me = lax.axis_index("col")
     width = pk.shape[2]
     share, span = top_s.shape
-    cand, _, _, picked, rank = merge(LEVELS, leaf, pk, pp, sp, skel_ref, rank_ref)
+    ranks = [meta[1 + i : 2 + i, 0:1] for i in range(3)]
+    cand, _, _, picked = merge(meta[0:1, :], ranks, pk, pp, sp)
     pk3[...] = picked
     raw = mm(cand, picked, 1, 1, 3)
     back = mm(raw, jnp.concatenate([pp[0], pp[1]], 0), 0, 0)
-    ww3[...], scale = ridged(mm(picked, picked, 1, 1, 3), rank)
+    ww3[...], scale = ridged(mm(picked, picked, 1, 1, 3), ranks[2])
     spd_inverse(ww3, scale, lambda b: None)
     turn = lax.rem(width - me * span, width)
     rows = pl.ds(pl.multiple_of(lax.rem(leaf, 8) * share, share), share)
@@ -175,7 +170,7 @@
 
 def hss_kernel(
     points_hbm, ids_hbm, signs_hbm, had_hbm, samp_hbm, skel_hbm, rank_hbm,
-    basis_ref, pk_out, sp_out, pp,
+    basis_ref, pk_out, sp_out, pp, meta,
     points_ref, ids_ref, signs_ref, had_ref, skel_ref, rank_ref, samp, every, om_all, own_b, pick_b, res, raw_ref, part, half, mine, landed, spk, pk_low, sp_low, hh, ww,
     samp_sem, g_s, g_r, gp_s, gp_r, p_s, p_r, pp_s, pp_r,
     pair_s, pair_r, rs_s, rs_r, ag_s, ag_r, ap_s, ap_r, ax_s, ax_r, axp_s, axp_r,
@@ -435,7 +430,7 @@
         scatter.append(put(mine.at[piece], landed.at[off - 1], rs_s.at[off], rs_r.at[off], col=zpeer(off) * 2 + core))
 
     def leaf_hook(b):
-        @pl.when(b == 2)
+        @pl.when(b == 0)
         def _():
             pair.wait_recv()
             mine[...] = part[pl.ds(own0, r2)] + half[...]
@@ -486,9 +481,15 @@
         put(got, got, axp_s.at[off], axp_r.at[off], keep=False, col=partner).wait_recv()
     pp[1 - side0] = mm(ww[0, 1 - side0], hh[0, 1 - side0], 1, 0)
 
+    row, ranks = node_of(LEVELS, leaf, skel_ref, rank_ref)
+    meta[0:1, :] = row
+    for i in range(3):
+        meta[1 + i : 2 + i, :] = jnp.broadcast_to(ranks[i], (1, r)).astype(jnp.int32)
+
     for level in range(1, LEVELS):
         side = sides[level]
-        cand, spots, chooser, picked, rank = merge(level, leaf, pk[level - 1], pp, sp[level - 1], skel_ref, rank_ref)
+        row, ranks = node_of(level, leaf, skel_ref, rank_ref)
+        cand, spots, chooser, picked = merge(row, ranks, pk[level - 1], pp, sp[level - 1])
         pk[level][side] = picked
         offer_picked(level)
         sp[level][side] = exact(spots, chooser, 1, 0)
@@ -496,7 +497,7 @@
         raw = mm(cand, picked, 1, 1, 3)
         hh[level, side] = mm(raw, jnp.concatenate([pp[0], pp[1]], 0), 0, 0)
         offer(hh, level, 4, xh_s, xh_r)
-        ww[level, side], scale = ridged(mm(picked, picked, 1, 1, 3), rank)
+        ww[level, side], scale = ridged(mm(picked, picked, 1, 1, 3), ranks[2])
 
         def hook(b, level=level):
             @pl.when(b == 5)
@@ -545,16 +546,17 @@
         DMA((7,)), *[DMA((ZS,))] * 8, DMA(()), DMA(()), *[DMA((ZS,))] * 10, *[DMA((LEVELS,))] * 2,
         *pair_of, *[DMA((LEVELS, 4))] * 4, *pair_of,
     ]
-    basis, pk, sp, pp = pl.pallas_call(
+    basis, pk, sp, pp, meta = pl.pallas_call(
         hss_kernel,
         out_shape=[
             shape((rows, r), BF16),
             shape((2, r, width), F32),
             shape((2, 8, r), F32),
             shape((2, r, width), F32),
+            shape((8, r), jnp.int32),
         ],
         in_specs=[HBM] * 7,
-        out_specs=[VM] * 4,
+        out_specs=[VM] * 5,
         scratch_shapes=[
             fetched((3, rows), F32),
             fetched((1, rows), jnp.int32),
@@ -589,18 +591,16 @@
     return pl.pallas_call(
         top_kernel,
         out_shape=[shape((rows, r), BF16), top, top],
-        in_specs=[VM, VM, VM, VM, HBM, HBM],
+        in_specs=[VM] * 5,
         out_specs=[ANY, VM, VM],
         scratch_shapes=[
-            fetched(skeleton.shape, jnp.int32),
-            pltpu.SMEM(ranks.shape, jnp.int32),
             fetched((r, width), F32),
             fetched((r, r), F32),
-            DMA((3,)),
+            DMA(()),
         ],
         compiler_params=pltpu.CompilerParams(vmem_limit_bytes=32 * 1024 * 1024),
         name="top",
-    )(basis, pk, pp, sp, *[pltpu.with_memory_space_constraint(x, pltpu.HBM) for x in (skeleton, ranks)])
+    )(basis, pk, pp, sp, meta)
 
 
 def solution(mesh):

time: 90.4 us -> 87.8 us (0.971)
  Pallas kernels: 89.6 us -> 87 us
    pallas_call x1, Pallas kernels: 81.2 us -> 79.4 us  [local(): pl.pallas_call(hss_kernel, out_shape=[shape((rows, r), BF16), shape((2, r...]
where the time goes in v8:
time: 87.8 us; the launch traced here: 87.6 us
  Pallas kernels  87 us (99%)
    pallas_call x1, Pallas kernels, local(): pl.pallas_call(hss_kernel, out_shape=[shape((rows, r), BF16), shape((2, r...  79.4 us
    pallas_call x1, Pallas kernels, local(): pl.pallas_call(top_kernel, out_shape=[shape((rows, r), BF16), top, top],...  7.62 us

profile of v8, /device:TPU:1, one launch (start us, length us, event | category | flops | bytes accessed | tf_op | source)
XLA Modules:
  0.0 87.6 jit_solution(12430248271972464570)
XLA Ops:
  0.6 79.4 %hss.1 = (bf16[512,128]{1,0:T(8,128)(2,1)S(1)}, f32[2,128,512]{2,1,0:T(8,128)S(1)}, f32[2,8,128]{2,1,0:T(8,128)S(1)}, f32[2,128,512]{2,1,0:T(8,128)S(1)}, s32[8,128]{1,0:T(8,128)S(1)}) custom-call(f32[3,512]{1,0:T(4,128)} %points_hbm.1, s32[1,512]{1,0:T(1,128)} %bitcast.3, s32[1,512]{1,0:T(1,128)} %bitcast.4, s32[1,512]{1,0:T(1,128)} %bitcast.5, ...), custom_call_target="tpu_custom_call" | custom-call | tf_op jit(solution)/shard_map/hss/pallas_call | solution.py:549
  80.0 7.6 %top.1 = (bf16[512,128]{1,0:T(8,128)(2,1)}, f32[16,32]{1,0:T(8,128)}, f32[16,32]{1,0:T(8,128)}) custom-call(bf16[512,128]{1,0:T(8,128)(2,1)S(1)} %get-tuple-element.8.basis_ref, f32[2,128,512]{2,1,0:T(8,128)S(1)} %get-tuple-element.9.pk, f32[2,128,512]{2,1,0:T(8,128)S(1)} %get-tuple-element.10.pp, f32[2,8,128]{2,1,0:T(8,128)S(1)} %get-tuple-element.11.sp, ...), custom_call_target="tpu_custom_call" | custom-call | tf_op jit(solution)/shard_map/top/pallas_call | solution.py:591

commit v9 on v8

--- a/solution.py
+++ b/solution.py
@@ -25,6 +25,7 @@
 ZS = COLS // 2
 LANES = 128
 LEVELS = 3
+FAR_FIRST = (4, 3, 5, 2, 6, 1, 7)
 
 
 def bdot(a, b, ca, cb):
@@ -434,8 +435,8 @@
         def _():
             pair.wait_recv()
             mine[...] = part[pl.ds(own0, r2)] + half[...]
-            for copy in scatter:
-                copy.start()
+            for off in FAR_FIRST:
+                scatter[off - 1].start()
 
         @pl.when(b == 6)
         def _():
@@ -454,7 +455,7 @@
         total = total + landed[off - 1]
     hh[0, side0, pl.ds(pl.multiple_of(own0 + z * count, count), count)] = total
     here = n_rows(side0, core, z)
-    for off in (1, 7, 2, 6, 3, 5, 4):
+    for off in FAR_FIRST:
         put(here, here, ag_s.at[off], ag_r.at[ZS - off], col=zpeer(off) * 2 + core).start()
     put(here, here, ap_s.at[0], ap_r.at[0], col=partner).start()
     put(here, here, ax_s.at[0], ax_r.at[0], leaf=siblings[0]).start()

time: 87.8 us -> 86.6 us (0.986)
  Pallas kernels: 87 us -> 85.8 us
    pallas_call x1, Pallas kernels: 79.4 us -> 78.2 us  [local(): pl.pallas_call(hss_kernel, out_shape=[shape((rows, r), BF16), shape((2, r...]
where the time goes in v9:
time: 86.6 us; the launch traced here: 86.4 us
  Pallas kernels  85.8 us (99%)
    pallas_call x1, Pallas kernels, local(): pl.pallas_call(hss_kernel, out_shape=[shape((rows, r), BF16), shape((2, r...  78.2 us
    pallas_call x1, Pallas kernels, local(): pl.pallas_call(top_kernel, out_shape=[shape((rows, r), BF16), top, top],...  7.61 us

profile of v9, /device:TPU:1, one launch (start us, length us, event | category | flops | bytes accessed | tf_op | source)
XLA Modules:
  0.0 86.4 jit_solution(7863126961454865144)
XLA Ops:
  0.6 78.2 %hss.1 = (bf16[512,128]{1,0:T(8,128)(2,1)S(1)}, f32[2,128,512]{2,1,0:T(8,128)S(1)}, f32[2,8,128]{2,1,0:T(8,128)S(1)}, f32[2,128,512]{2,1,0:T(8,128)S(1)}, s32[8,128]{1,0:T(8,128)S(1)}) custom-call(f32[3,512]{1,0:T(4,128)} %points_hbm.1, s32[1,512]{1,0:T(1,128)} %bitcast.3, s32[1,512]{1,0:T(1,128)} %bitcast.4, s32[1,512]{1,0:T(1,128)} %bitcast.5, ...), custom_call_target="tpu_custom_call" | custom-call | tf_op jit(solution)/shard_map/hss/pallas_call | solution.py:550
  78.8 7.6 %top.1 = (bf16[512,128]{1,0:T(8,128)(2,1)}, f32[16,32]{1,0:T(8,128)}, f32[16,32]{1,0:T(8,128)}) custom-call(bf16[512,128]{1,0:T(8,128)(2,1)S(1)} %get-tuple-element.8.basis_ref, f32[2,128,512]{2,1,0:T(8,128)S(1)} %get-tuple-element.9.pk, f32[2,128,512]{2,1,0:T(8,128)S(1)} %get-tuple-element.10.pp, f32[2,8,128]{2,1,0:T(8,128)S(1)} %get-tuple-element.11.sp, ...), custom_call_target="tpu_custom_call" | custom-call | tf_op jit(solution)/shard_map/top/pallas_call | solution.py:592
